TPU v7x, 32 devices: a whole 2x2x4 slice. The times are simulated.
32 devices in a mesh: dp: 8 (over y, x, core), seq: 4 (over z).
Axes of the slice: x: 2, y: 2, z: 4, core: 2. Of those that a mesh axis runs over, the one named last changes fastest.
Arguments:
- tokens: bfloat16 [2, 8, 1024, 768], P(None, 'dp', 'seq'), may hold values from -6 to 6
- lengths: int32 [2, 8], P(None, 'dp'), may hold values from 256 to 1024, as said below
- dealing: int32 [2, 8], P(None, 'dp'), may hold values from 0 to 7, each once within a row
- cotangent: bfloat16 [2, 8, 1024, 768], P(None, 'dp', 'seq'), may hold values from -6 to 6
- in_weight: bfloat16 [768, 3352], P(('dp', 'seq')), may hold values from -0.21875 to 0.21875
- out_weight: bfloat16 [1536, 768], P(('dp', 'seq')), may hold values from -0.15625 to 0.15625
- norm_gain: bfloat16 [768], P(('dp', 'seq')), may hold values from 0.5 to 1.5
- gate_gain: bfloat16 [1536], P(('dp', 'seq')), may hold values from 0.5 to 1.5
- conv_weight: float32 [4, 1792], replicated, may hold values from -3 to 3
- conv_bias: float32 [1792], replicated, may hold values from -0.5 to 0.5
- decay_log: float32 [24], replicated, may hold values from -5 to 1
- step_bias: float32 [24], replicated, may hold values from -4 to -2
- skip_gain: float32 [24], replicated, may hold values from 0.5 to 1.5
Outputs:
- outputs: bfloat16 [2, 8, 1024, 768], P(None, 'dp', 'seq')
- grad_tokens: bfloat16 [2, 8, 1024, 768], P(None, 'dp', 'seq')
- grad_in_weight: float32 [768, 3352], P(('dp', 'seq'))
- grad_out_weight: float32 [1536, 768], P(('dp', 'seq'))
- grad_norm_gain: float32 [768], P(('dp', 'seq'))
- grad_gate_gain: float32 [1536], P(('dp', 'seq'))
- grad_conv_weight: float32 [4, 1792], replicated
- grad_conv_bias: float32 [1792], replicated
- grad_decay_log: float32 [24], replicated
- grad_step_bias: float32 [24], replicated
- grad_skip_gain: float32 [24], replicated
Inputs may be any that keep to these rules, and one draw needn't show every extreme that they name: `lengths`: in every draw one sequence has exactly 1024 valid tokens and one exactly 256. Each row of dealing names every slot of its micro-batch once.
All inputs are finite; a program needn't handle non-finite values.
Results may differ from a plain program's by a relative error of at most 0.0075.
Values may be sent and summed in bfloat16 or wider, within the bound.
No kernel may reach another device: no remote copies, remote signals or barrier semaphores. Data moves between devices by JAX's collectives and lax.ppermute only.
A program may use at most 192 MiB of HBM per device.

v0:
```python
import functools

import jax
import jax.numpy as jnp
from jax import lax
from jax.experimental import pallas as pl
from jax.experimental.pallas import tpu as pltpu
from jax.sharding import PartitionSpec as P

INNER = 1536
HEADS = 24
HDIM = 64
STATE = 128
KCONV = 4
CHANNELS = INNER + 2 * STATE
LANES = 128
CHUNK = 128
HALO = 16
PIECES = 4
EPSILON = 1e-05
WIDTH = CHANNELS + LANES
F32 = jnp.float32
BF16 = jnp.bfloat16
BOTH = ("dp", "seq")
VMEM_LIMIT = 60 * 1024 * 1024


def flip_dp(value, mask):
    pairs = [(i, i ^ mask) for i in range(lax.axis_size("dp"))]
    return lax.ppermute(value, "dp", pairs)


def step_bits(size):
    return list(range(1, size.bit_length() - 1))


def flip_step(value, step):
    size = lax.axis_size("dp")
    bits = step_bits(size)
    pairs = [(i, i ^ (1 << (bits[-1 - step] if i % 2 else bits[step]))) for i in range(size)]
    return lax.ppermute(value, "dp", pairs)


def shift_seq(value, step):
    size = lax.axis_size("seq")
    return lax.ppermute(value, "seq", [(i, (i + step) % size) for i in range(size)])


def column_place(dp_even, lin):
    return (dp_even + lin % 2) * lax.axis_size("seq") + lin // 2


def unit_pairs(parity):
    size = lax.axis_size("seq")
    pairs = []
    for dp in range(lax.axis_size("dp")):
        core = dp % 2
        for block in range(size):
            micro = (block % 2) ^ parity
            lin = (2 * micro + core) * (size // 2) + block // 2
            pairs.append((dp * size + block, column_place(dp - core, lin)))
    return pairs


def neighbour_pairs(step):
    size = lax.axis_size("seq")
    group = size // 2
    pairs = []
    for dp_even in range(0, lax.axis_size("dp"), 2):
        for lin in range(2 * size):
            if 0 <= lin % group + step < group:
                pairs.append((column_place(dp_even, lin), column_place(dp_even, lin + step)))
    return pairs


def reversed_pairs(pairs):
    return [(target, source) for source, target in pairs]


def to_stretch(blocks, place):
    odd = place["seq"] % 2 == 1
    first = lax.ppermute(jnp.where(odd, blocks[1], blocks[0]), BOTH, unit_pairs(0))
    second = lax.ppermute(jnp.where(odd, blocks[0], blocks[1]), BOTH, unit_pairs(1))
    return first, second


def swapped(swap, pair):
    return jnp.where(swap, pair[1], pair[0]), jnp.where(swap, pair[0], pair[1])


def from_stretch(first, second, place):
    late = place["micro"] == 1
    one = lax.ppermute(jnp.where(late, second, first), BOTH, reversed_pairs(unit_pairs(0)))
    two = lax.ppermute(jnp.where(late, first, second), BOTH, reversed_pairs(unit_pairs(1)))
    return one, two


class Chain:
    def __init__(self, stages):
        self.stages = stages
        self.value = None
        self.pending = next(stages)

    def feed(self, arrived):
        try:
            self.pending = self.stages.send(arrived)
        except StopIteration as stop:
            self.pending = None
            self.value = stop.value


def advance(held, *chains):
    moving = [chain for chain in chains if chain.pending is not None]
    held, arrived = lax.optimization_barrier((held, [chain.pending for chain in moving]))
    for chain, got in zip(moving, arrived):
        chain.feed(got)
    return held


def seq_shifts(shard):
    return [shift_seq(shard, j) for j in range(1, lax.axis_size("seq"))]


def seq_order(shard, arrived, place):
    size = lax.axis_size("seq")
    got = [shard] + list(arrived)
    rows = []
    for i in range(size):
        row = got[0]
        for j in range(1, size):
            row = jnp.where((place["seq"] - i) % size == j, got[j], row)
        rows.append(row)
    return jnp.stack(rows)


def seq_stages(shard, place):
    arrived = yield seq_shifts(shard)
    return seq_order(shard, arrived, place)


def spread_stages(block):
    steps = len(step_bits(lax.axis_size("dp")))
    held, last, turned = block[None], None, None
    for step in range(steps):
        if last is not None:
            held = jnp.concatenate([held, last])
        if step < steps - 1:
            last = (yield [flip_step(held, step)])[0]
        else:
            last, turned = yield [flip_step(held, step), flip_dp(held, 1)]
    end = (yield [flip_dp(last, 1)])[0]
    return [held, last, turned, end]


def spread_masks(size):
    found = []
    for bits in (step_bits(size), step_bits(size)[::-1]):
        masks, last = (0,), None
        for bit in bits:
            if last is not None:
                masks = masks + last
            last = tuple(m ^ (1 << bit) for m in masks)
        found.append((masks, last))
    even, odd = found
    own = [(even[n], odd[n]) for n in range(2)]
    return own + [(tuple(m ^ 1 for m in b), tuple(m ^ 1 for m in a)) for a, b in own]


def reduce_stages(keep, send, place, take):
    steps = len(step_bits(lax.axis_size("dp")))
    got = yield [flip_dp(send, 1)]
    parts = [part.reshape((2,) * steps + part.shape[1:]) for part in (keep, got[0])]
    for step in range(steps):
        got = yield [flip_step(add_up([part[1] for part in parts]).astype(BF16), step)]
        parts = [part[0] for part in parts] + got
    size = lax.axis_size("seq")

    def rows_for(j):
        return add_up([take(part, (place["seq"] + j) % size) for part in parts])

    moved = yield [shift_seq(rows_for(j).astype(BF16), j) for j in range(1, size)]
    return add_up([rows_for(0)] + moved)


def add_up(parts):
    total = parts[0].astype(F32)
    for part in parts[1:]:
        total = total + part.astype(F32)
    return total


def sum_stages(value):
    value = value + flip_dp(value, 1)
    size = lax.axis_size("seq")
    apart = 1
    while apart < size:
        got = yield [lax.ppermute(value, "seq", [(i, i ^ apart) for i in range(size)])]
        value = value + got[0]
        apart *= 2
    for bit in range(1, lax.axis_size("dp").bit_length() - 1):
        got = yield [flip_dp(value, 1 << bit)]
        value = value + got[0]
    return value


def dp_table(row):
    table = row[None]
    for bit in range(lax.axis_size("dp").bit_length() - 1):
        table = jnp.concatenate([table, flip_dp(table, 1 << bit)])
    return table


def route_row(dp, goal, first_bit, second_bit):
    held = [0, 1, first_bit, first_bit | 1]

    def chosen(base):
        low = jnp.int32(0)
        high = jnp.int32(0)
        for n in range(3, -1, -1):
            away = jnp.bitwise_xor(goal[base ^ held[n]], jnp.bitwise_xor(dp, base))
            cross = (jnp.bitwise_and(away, second_bit) != 0) & (jnp.bitwise_and(away, first_bit) == 0)
            low = jnp.where(cross, n, low)
        for n in range(4):
            away = jnp.bitwise_xor(goal[base ^ held[n]], jnp.bitwise_xor(dp, base))
            cross = (jnp.bitwise_and(away, second_bit) != 0) & (jnp.bitwise_and(away, first_bit) == 0)
            high = jnp.where(cross, n, high)
        return low, high

    low, high = chosen(0)
    other_low, _ = chosen(second_bit)
    row = [low, high]
    for side in range(2):
        pick = jnp.int32(0)
        target = jnp.bitwise_xor(dp, side)
        for n in range(4):
            pick = jnp.where(goal[held[n]] == target, n, pick)
            far = jnp.where(other_low == n, 4, 5)
            pick = jnp.where(goal[held[n] ^ second_bit] == target, far, pick)
        row.append(pick)
    return row


def route_kernel(place_ref, table_ref, out_ref):
    dp = place_ref[0]
    size = table_ref.shape[0]
    for way in range(2):
        for micro in range(2):
            goal = []
            for r in range(size):
                if way == 1:
                    goal.append(table_ref[r, micro])
                else:
                    found = jnp.int32(0)
                    for other in range(size):
                        hit = table_ref[other, micro] == jnp.bitwise_xor(dp, r)
                        found = jnp.where(hit, jnp.bitwise_xor(dp, other), found)
                    goal.append(found)
            even = route_row(dp, goal, 2, 4)
            odd = route_row(dp, goal, 4, 2)
            for n in range(4):
                out_ref[way * 2 + micro, n] = jnp.where(jnp.bitwise_and(dp, 1) == 0, even[n], odd[n])
    core = jnp.bitwise_and(dp, 1)
    column = jnp.bitwise_xor(core, place_ref[2])
    micro = place_ref[1]
    own = jnp.where(micro == 0, table_ref[0, 2], table_ref[0, 3])
    other = jnp.where(micro == 0, table_ref[1, 2], table_ref[1, 3])
    out_ref[4, 0] = jnp.where(column == 0, own, other)
    out_ref[4, 1] = place_ref[3]
    for n in range(2, 4):
        out_ref[4, n] = jnp.int32(0)


def make_routes(place, table):
    return pl.pallas_call(
        route_kernel,
        out_shape=jax.ShapeDtypeStruct((5, 4), jnp.int32),
        in_specs=[pl.BlockSpec(memory_space=pltpu.SMEM)] * 2,
        out_specs=pl.BlockSpec(memory_space=pltpu.SMEM),
    )(jnp.stack([place["dp"], place["micro"], place["column"], place["seq"] % 2]), table)


def pick_entries(index, entries, out, also=True):
    for n, entry in enumerate(entries):

        @pl.when((index == n) & also)
        def _():
            out[...] = entry[...]


def entries_of(micro, refs):
    return [ref.at[micro, n] for ref in refs for n in range(2)]


def pick_sent_kernel(first, route_ref, pair_ref, came_ref, sent_ref):
    for micro in range(2):
        for k in range(2):
            entries = entries_of(micro, (pair_ref, came_ref))
            pick_entries(route_ref[first + micro, k], entries, sent_ref.at[micro, k])


def pick_last_kernel(first, route_ref, pair_ref, came_ref, far_ref, own_ref, partner_ref):
    for micro in range(2):
        entries = entries_of(micro, (pair_ref, came_ref, far_ref))
        for k, out_ref in enumerate((own_ref, partner_ref)):
            pick_entries(route_ref[first + micro, 2 + k], entries, out_ref.at[micro])


def pick(body, routes, shapes, *held):
    vmem = pl.BlockSpec(memory_space=pltpu.VMEM)
    return pl.pallas_call(
        body,
        out_shape=[jax.ShapeDtypeStruct(shape, BF16) for shape in shapes],
        in_specs=[pl.BlockSpec(memory_space=pltpu.SMEM)] + [vmem] * len(held),
        out_specs=[vmem] * len(shapes),
    )(routes, *held)


def core_pair(items, place):
    low_core = place["dp"] % 2 == 0
    half = items.shape[1] // 2
    mine, give = swapped(jnp.logical_not(low_core), (items[:, :half], items[:, half:]))
    return jnp.stack([mine, flip_dp(give, 1)], axis=1)


def cotangent_stages(pair, routes, place):
    low_core = place["dp"] % 2 == 0
    pair = (yield [pair])[0]
    came = (yield [flip_step(pair, 0)])[0]
    (sent,) = yield pick(functools.partial(pick_sent_kernel, 0), routes, [pair.shape], pair, came)
    far = flip_step(sent, 1)
    yield []
    far = (yield [far])[0]
    body = functools.partial(pick_last_kernel, 0)
    own, partner = pick(body, routes, [pair[:, 0].shape] * 2, pair, came, far)
    blocks = jnp.concatenate(swapped(jnp.logical_not(low_core), (own, flip_dp(partner, 1))), axis=1)
    one, two = to_stretch(blocks, place)
    one = (yield [one])[0]
    two = (yield [two])[0]
    return jnp.concatenate(swapped(place["micro"] == 1, (one, two)))


def output_stages(out, routes, place):
    block = out.shape[0] // 2
    one, two = from_stretch(out[:block], out[block:], place)
    one = (yield [one])[0]
    two = (yield [two])[0]
    blocks = jnp.stack(swapped(place["seq"] % 2 == 1, (one, two)))
    tops, bottoms = blocks[:, : block // 2], blocks[:, block // 2 :]
    mine, give = swapped(place["dp"] % 2 == 1, (tops, bottoms))
    got = (yield [flip_dp(give, 1)])[0]
    pair = jnp.stack([mine, got], axis=1)
    came = (yield [flip_step(pair, 0)])[0]
    (sent,) = pick(functools.partial(pick_sent_kernel, 2), routes, [pair.shape], pair, came)
    far = (yield [flip_step(sent, 1)])[0]
    body = functools.partial(pick_last_kernel, 2)
    own, partner = pick(body, routes, [mine.shape] * 2, pair, came, far)
    back = (yield [flip_dp(partner, 1)])[0]
    return jnp.concatenate(swapped(place["dp"] % 2 == 1, (own, back)), axis=1)


def deal_gathered(items, source):
    every = lax.all_gather(items, "dp", axis=0)
    picked = [
        lax.dynamic_index_in_dim(every[:, m], source[m], 0, keepdims=False) for m in range(2)
    ]
    return jnp.stack(picked)


def dot(a, b, ca=1, cb=0):
    return lax.dot_general(a, b, (((ca,), (cb,)), ((), ())), preferred_element_type=F32)


def two_parts(x):
    high = x.astype(BF16)
    return high, (x - high.astype(F32)).astype(BF16)


def running_sum(x, reverse=False):
    rows = lax.broadcasted_iota(jnp.int32, (CHUNK, CHUNK), 0)
    cols = lax.broadcasted_iota(jnp.int32, (CHUNK, CHUNK), 1)
    reach = (rows <= cols) if reverse else (rows >= cols)
    reach = jnp.where(reach, 1.0, 0.0).astype(BF16)
    high, rest = two_parts(x)
    middle, low = two_parts(x - high.astype(F32))
    del rest
    return dot(reach, high) + dot(reach, middle) + dot(reach, low)


def fill_expander(expand_ref):
    head = lax.broadcasted_iota(jnp.int32, (LANES, INNER), 0)
    col = lax.broadcasted_iota(jnp.int32, (LANES, INNER), 1)
    one = jnp.where(col // HDIM == head, 1.0, 0.0).astype(BF16)
    expand_ref[0:LANES, :] = one
    expand_ref[LANES : 2 * LANES, :] = one


def head_sums(prod, tile):
    lane = lax.broadcasted_iota(jnp.int32, (LANES, LANES), 0)
    head = lax.broadcasted_iota(jnp.int32, (LANES, LANES), 1)
    one = jnp.where(2 * tile + lane // HDIM == head, 1.0, 0.0).astype(BF16)
    high, low = two_parts(prod)
    return dot(jnp.concatenate([high, low], axis=1), jnp.concatenate([one, one], axis=0))


def start_pieces(dp, pieces, plan, target, sem, rows):
    copies = []
    masks, spots = plan
    for piece, (even, odd) in zip(pieces, masks):
        for n in range(len(even)):
            mask = jnp.where(jnp.bitwise_and(dp, 1) == 0, even[n], odd[n])
            for source, scale, source_col, col, width in spots:
                first = pl.multiple_of(jnp.bitwise_xor(dp, mask) * (rows * scale), 8)
                copy = pltpu.make_async_copy(
                    piece.at[n, pl.ds(source, rows * scale), pl.ds(source_col, width)],
                    target.at[pl.ds(first, rows * scale), pl.ds(col, width)],
                    sem.at[len(copies)],
                )
                copy.start()
                copies.append(copy)
    return copies


def wait_all(copies):
    for copy in copies:
        copy.wait()


def piece_count(plan):
    masks, spots = plan
    return sum(len(even) for even, _ in masks) * len(spots)


def gain_row(w_ref):
    return w_ref[:, CHANNELS:].astype(F32).T[HEADS : HEADS + 1]


def project_kernel(plan, rows, scal, x_ref, cw_ref, cb_ref, dl_ref, sb_ref, *refs):
    count = PIECES
    pieces = refs[:count]
    nh_ref, cext_ref, act_ref, step_ref, sig_ref, cum_ref = refs[count : count + 6]
    w_ref, proj_ref, sem = refs[count + 6 :]
    copies = start_pieces(scal[0], pieces, plan, w_ref, sem, rows)
    total = x_ref.shape[0]
    length = total - HALO
    chunks = length // CHUNK

    tall = 3 * HALO if total % (3 * HALO) == 0 else HALO

    def norm(i, carry):
        at = pl.ds(pl.multiple_of(i * tall, tall), tall)
        u = x_ref[at, :].astype(F32)
        scale = lax.rsqrt(jnp.mean(u * u, axis=1, keepdims=True) + EPSILON)
        nh_ref[at, :] = (u * scale * gain).astype(BF16)
        return carry

    wait_all(copies)
    gain = gain_row(w_ref)
    lax.fori_loop(0, total // tall, norm, 0)

    def project(j, carry):
        at = pl.ds(pl.multiple_of(j * 384, 384), 384)
        proj_ref[:, at] = dot(nh_ref[...], w_ref[:, at])
        return carry

    lax.fori_loop(0, WIDTH // 384, project, 0)

    def conv(idx, carry):
        i, j = idx // (CHANNELS // LANES), idx % (CHANNELS // LANES)
        cols = pl.ds(pl.multiple_of(j * LANES, LANES), LANES)
        first = pl.multiple_of(i * CHUNK, CHUNK)
        part = proj_ref[pl.ds(first, CHUNK + HALO), cols]
        weights = cw_ref[:, cols]
        out = cb_ref[0:1, cols] + weights[KCONV - 1 : KCONV] * part[HALO:]
        for k in range(KCONV - 1):
            out = out + weights[k : k + 1] * pltpu.roll(part, KCONV - 1 - k, 0)[HALO:]
        act_ref[pl.ds(first, CHUNK), cols] = (out * jax.nn.sigmoid(out)).astype(BF16)
        cext_ref[pl.ds(first + HALO, CHUNK), cols] = part[HALO:].astype(BF16)
        return carry

    lax.fori_loop(0, chunks * (CHANNELS // LANES), conv, 0)
    cext_ref[0:HALO, :] = proj_ref[0:HALO, 0:CHANNELS].astype(BF16)
    lane = lax.broadcasted_iota(jnp.int32, (CHUNK, LANES), 1)
    row = lax.broadcasted_iota(jnp.int32, (CHUNK, LANES), 0)
    rate = -jnp.exp(dl_ref[0:1, :])
    for i in range(chunks):
        at = pl.ds(i * CHUNK, CHUNK)
        pre = proj_ref[pl.ds(HALO + i * CHUNK, CHUNK), pl.ds(CHANNELS, LANES)] + sb_ref[0:1, :]
        live = (row + i * CHUNK < scal[1]) & (lane < HEADS)
        soft = jnp.maximum(pre, 0.0) + jnp.log1p(jnp.exp(-jnp.abs(pre)))
        step = jnp.where(live, soft, 0.0)
        step_ref[at, :] = step
        sig_ref[at, :] = jnp.where(live, jax.nn.sigmoid(pre), 0.0)
        cum_ref[at, :] = running_sum(rate * step)


def mixing_parts(cum, cum_rows, step_rows, head):
    gap = jnp.minimum(cum[:, head : head + 1] - cum_rows[head : head + 1, :], 0.0)
    return jnp.exp(gap) * step_rows[head : head + 1, :]


def causal_tile():
    rows = lax.broadcasted_iota(jnp.int32, (CHUNK, CHUNK), 0)
    cols = lax.broadcasted_iota(jnp.int32, (CHUNK, CHUNK), 1)
    return rows >= cols


def local_kernel(act_ref, step_ref, cum_ref, local_ref, upd_ref, tot_ref, sum_ref, expand_ref):
    chunks = act_ref.shape[0] // CHUNK
    left = lax.broadcasted_iota(jnp.int32, (CHUNK, LANES), 1) < HDIM
    fill_expander(expand_ref)
    after = jnp.zeros((1, LANES), F32)
    for i in range(chunks - 1, -1, -1):
        at = pl.ds(i * CHUNK, CHUNK)
        cum = cum_ref[at, :]
        last = cum[CHUNK - 1 : CHUNK]
        weight = jnp.exp(last + after - cum) * step_ref[at, :]
        wide = dot(jnp.concatenate(two_parts(weight), axis=1), expand_ref[...])
        values = act_ref[at, 0:INNER].astype(F32)
        keys = act_ref[at, INNER : INNER + STATE]
        update = dot(keys, (wide * values).astype(BF16), 0, 0)
        sum_ref[...] = update if i == chunks - 1 else sum_ref[...] + update
        after = after + last
    upd_ref[...] = sum_ref[...].astype(BF16)
    tot_ref[...] = jnp.broadcast_to(after, tot_ref.shape)

    def chunk(c, carry):
        at = pl.ds(pl.multiple_of(c * CHUNK, CHUNK), CHUNK)
        in_keys = act_ref[at, INNER : INNER + STATE]
        out_keys = act_ref[at, INNER + STATE : CHANNELS]
        affinity = jnp.where(causal_tile(), dot(out_keys, in_keys, 1, 1), 0.0)
        cum = cum_ref[at, :]
        cum_rows = cum.T
        step_rows = step_ref[at, :].T
        for tile in range(INNER // LANES):
            cols = slice(tile * LANES, (tile + 1) * LANES)
            mixing = [
                (affinity * mixing_parts(cum, cum_rows, step_rows, 2 * tile + n)).astype(BF16)
                for n in range(2)
            ]
            values = act_ref[at, cols]
            zero = jnp.zeros_like(values)
            apart = jnp.concatenate(
                [jnp.where(left, values, zero), jnp.where(left, zero, values)], axis=0
            )
            local_ref[at, cols] = dot(jnp.concatenate(mixing, axis=1), apart)
        return carry

    lax.fori_loop(0, chunks, chunk, 0)


def middle_kernel(gate_plan, plan, rows, scal, local_ref, act_ref, step_ref, cum_ref, nh_ref, state_ref, x_ref,
                  c_ref, skip_ref, *refs):
    count = PIECES
    out_ref, gn_ref, dgate_ref, gcore_ref, rowq_ref, lsg_ref, states_ref, gskip_ref = refs[
        count : count + 8
    ]
    (w_ref, wg_ref, gate_ref, gain_ref, mc_ref, gno_ref, state_s, wide_ref, core_ref, mixed_ref, acc_ref, expand_ref,
     gate_sem, sem) = refs[count + 8 :]
    gate_copies = start_pieces(scal[0], refs[:count], gate_plan, wg_ref, gate_sem, rows)
    copies = start_pieces(scal[0], refs[:count], plan, w_ref, sem, rows)
    length = act_ref.shape[0]
    chunks = length // CHUNK
    tiles = INNER // LANES
    model = c_ref.shape[1]
    fill_expander(expand_ref)

    def mask(i, carry):
        at = pl.ds(pl.multiple_of(i * CHUNK, CHUNK), CHUNK)
        row = lax.broadcasted_iota(jnp.int32, (CHUNK, model), 0) + i * CHUNK
        c = c_ref[at, :]
        mc_ref[at, :] = jnp.where(row < scal[1], c.astype(F32), 0.0).astype(BF16)
        return carry

    lax.fori_loop(0, chunks, mask, 0)
    wait_all(gate_copies)

    def project(j, carry):
        at = pl.ds(pl.multiple_of(j * 384, 384), 384)
        gate_ref[:, at] = dot(nh_ref[HALO:, :], wg_ref[:, at])
        return carry

    lax.fori_loop(0, INNER // 384, project, 0)
    wait_all(copies)

    def back_project(j, carry):
        at = pl.ds(pl.multiple_of(j * 384, 384), 384)
        gno_ref[:, at] = dot(mc_ref[...], w_ref[at, 0:model], 1, 1)
        return carry

    lax.fori_loop(0, INNER // 384, back_project, 0)
    gain_ref[...] = w_ref[:, model:].astype(F32).T[0:8]
    state_s[...] = state_ref[...].astype(F32)
    acc_ref[...] = jnp.zeros_like(acc_ref)
    gskip_ref[...] = jnp.zeros_like(gskip_ref)

    def chunk(c, before):
        at = pl.ds(pl.multiple_of(c * CHUNK, CHUNK), CHUNK)
        in_keys = act_ref[at, INNER : INNER + STATE]
        out_keys = act_ref[at, INNER + STATE : CHANNELS]
        cum = cum_ref[at, :]
        last = cum[CHUNK - 1 : CHUNK]
        growth = jnp.exp(cum)
        weight = jnp.exp(last - cum) * step_ref[at, :]
        small = jnp.concatenate(
            [growth, weight, jnp.exp(cum + before), jnp.broadcast_to(jnp.exp(last), (8, LANES))], axis=0
        )
        wide_ref[...] = dot(jnp.concatenate(two_parts(small), axis=1), expand_ref[...])
        state_b = state_s[...].astype(BF16)
        states_ref[c] = state_b
        squares = jnp.zeros((CHUNK, LANES), F32)
        for tile in range(tiles):
            cols = slice(tile * LANES, (tile + 1) * LANES)
            values = act_ref[at, cols].astype(F32)
            readout = dot(out_keys, state_b[:, cols])
            core = local_ref[at, cols] + wide_ref[0:CHUNK, cols] * readout
            mixed = core + skip_ref[0:1, cols] * values
            core_ref[:, cols] = core
            mixed_ref[:, cols] = mixed
            gate = gate_ref[at, cols]
            gated = mixed * (gate * jax.nn.sigmoid(gate))
            squares = squares + gated * gated
            weighted = (wide_ref[CHUNK : 2 * CHUNK, cols] * values).astype(BF16)
            state_s[:, cols] = wide_ref[3 * CHUNK : 3 * CHUNK + 1, cols] * state_s[:, cols] + dot(
                in_keys, weighted, 0, 0
            )
        scale = lax.rsqrt(jnp.sum(squares, axis=1, keepdims=True) / INNER + EPSILON)
        products = jnp.zeros((CHUNK, LANES), F32)
        for tile in range(tiles):
            cols = slice(tile * LANES, (tile + 1) * LANES)
            gate = gate_ref[at, cols]
            gn = mixed_ref[:, cols] * (gate * jax.nn.sigmoid(gate)) * scale
            gain = gain_ref[0:1, cols]
            gn_ref[at, cols] = (gn * gain).astype(BF16)
            products = products + gn * (gno_ref[at, cols] * gain)
        mean = jnp.sum(products, axis=1, keepdims=True) / INNER
        rowq = jnp.zeros((CHUNK, LANES), F32)
        for tile in range(tiles):
            cols = slice(tile * LANES, (tile + 1) * LANES)
            gate = gate_ref[at, cols]
            sig = jax.nn.sigmoid(gate)
            silu = gate * sig
            mixed = mixed_ref[:, cols]
            dgated = scale * (gno_ref[at, cols] * gain_ref[0:1, cols] - (mixed * silu * scale) * mean)
            g = dgated * silu
            dgate_ref[at, cols] = (dgated * mixed * (sig * (1.0 + gate * (1.0 - sig)))).astype(BF16)
            gcore = g.astype(BF16)
            gcore_ref[at, cols] = gcore
            values = act_ref[at, cols].astype(F32)
            gskip_ref[:, cols] = gskip_ref[:, cols] + jnp.sum(
                (g * values).reshape(CHUNK // 8, 8, LANES), axis=0
            )
            gcore_f = gcore.astype(F32)
            rowq = rowq + head_sums(gcore_f * core_ref[:, cols], tile)
            scaled = (wide_ref[2 * CHUNK : 3 * CHUNK, cols] * gcore_f).astype(BF16)
            acc_ref[:, cols] = acc_ref[:, cols] + dot(out_keys, scaled, 0, 0)
        rowq_ref[at, :] = rowq
        return before + last

    lax.fori_loop(0, chunks, chunk, jnp.zeros((1, LANES), F32))
    lsg_ref[...] = acc_ref[...].astype(BF16)

    def finish(i, carry):
        at = pl.ds(pl.multiple_of(i * CHUNK, CHUNK), CHUNK)
        row = lax.broadcasted_iota(jnp.int32, (CHUNK, model), 0) + i * CHUNK
        u = x_ref[pl.ds(pl.multiple_of(i * CHUNK + HALO, HALO), CHUNK), :].astype(F32)
        out_ref[at, :] = (u + jnp.where(row < scal[1], gno_ref[at, 0:model], 0.0)).astype(BF16)
        return carry

    for j in range(2):
        cols = slice(j * model // 2, (j + 1) * model // 2)
        gno_ref[:, cols] = dot(gn_ref[...], w_ref[:, cols])
    lax.fori_loop(0, chunks, finish, 0)


def put_block(dp, devices, block, keep_ref, send_ref, start, cols, part):
    steps = len(step_bits(devices))
    away = jnp.bitwise_xor(dp, block)
    backward = away // 2
    forward = jnp.int32(0)
    for k in range(steps):
        forward = forward * 2 + jnp.bitwise_and(jnp.right_shift(backward, k), 1)
    even = jnp.bitwise_and(dp, 1) == 0
    rows = part.shape[0]

    @pl.when(away % 2 == 0)
    def _():
        keep_ref[jnp.where(even, forward, backward), start : start + rows, cols] = part

    @pl.when(away % 2 == 1)
    def _():
        send_ref[jnp.where(even, backward, forward), start : start + rows, cols] = part


def early_kernel(rows, devices, scal, gn_ref, c_ref, nh_ref, dgate_ref, keep_ref, send_ref, mc_ref):
    length, model = c_ref.shape
    chunks = length // CHUNK

    def mask(i, carry):
        at = pl.ds(pl.multiple_of(i * CHUNK, CHUNK), CHUNK)
        row = lax.broadcasted_iota(jnp.int32, (CHUNK, model), 0) + i * CHUNK
        mc_ref[at, :] = jnp.where(row < scal[1], c_ref[at, :].astype(F32), 0.0).astype(BF16)
        return carry

    lax.fori_loop(0, chunks, mask, 0)
    half = model // 2
    for j in range(2 * INNER // model):
        part = dot(nh_ref[HALO:, :], dgate_ref[:, j * half : (j + 1) * half], 0, 0).astype(BF16)
        start = (j // 2) * rows
        cols = slice((j % 2) * half, (j % 2 + 1) * half)
        for block in range(devices):
            put_block(
                scal[0], devices, block, keep_ref, send_ref, start, cols, part[block * rows : (block + 1) * rows]
            )
    for j in range(INNER // half):
        part = dot(gn_ref[:, j * half : (j + 1) * half], mc_ref[...], 0, 0).astype(BF16)
        each = half // (2 * rows)
        for n in range(each):
            put_block(
                scal[0], devices, j * each + n, keep_ref, send_ref, 2 * rows, slice(0, model),
                part[n * 2 * rows : (n + 1) * 2 * rows],
            )


def local_back_kernel(plan, rows, scal, act_ref, step_ref, cum_ref, gcore_ref, dgate_ref, *refs):
    count = PIECES
    pieces = refs[:count]
    gvl_ref, gk_ref, gng_ref, w_ref, sem = refs[count:]
    copies = start_pieces(scal[0], pieces, plan, w_ref, sem, rows)
    chunks = act_ref.shape[0] // CHUNK
    half = gng_ref.shape[1] // 2
    left = lax.broadcasted_iota(jnp.int32, (CHUNK, LANES), 1) < HDIM

    def chunk(c, carry):
        at = pl.ds(pl.multiple_of(c * CHUNK, CHUNK), CHUNK)
        in_keys = act_ref[at, INNER : INNER + STATE]
        out_keys = act_ref[at, INNER + STATE : CHANNELS]
        affinity = jnp.where(causal_tile(), dot(out_keys, in_keys, 1, 1), 0.0)
        cum = cum_ref[at, :]
        cum_rows = cum.T
        step_rows = step_ref[at, :].T
        gaff = jnp.zeros((CHUNK, CHUNK), F32)
        for tile in range(INNER // LANES):
            cols = slice(tile * LANES, (tile + 1) * LANES)
            values = act_ref[at, cols]
            grads = gcore_ref[at, cols]
            zero = jnp.zeros_like(grads)
            apart = jnp.concatenate(
                [jnp.where(left, grads, zero), jnp.where(left, zero, grads)], axis=0
            )
            gmix = dot(apart, values, 1, 1)
            mixing = []
            for n in range(2):
                weight = mixing_parts(cum, cum_rows, step_rows, 2 * tile + n)
                gaff = gaff + gmix[n * CHUNK : (n + 1) * CHUNK] * weight
                mixing.append((affinity * weight).astype(BF16))
            back = dot(jnp.concatenate(mixing, axis=1), grads, 0, 0)
            gvl_ref[at, cols] = jnp.where(left, back[0:CHUNK], back[CHUNK:])
        gaff = jnp.where(causal_tile(), gaff, 0.0).astype(BF16)
        gk_ref[at, 0:STATE] = dot(gaff, out_keys, 0, 0)
        gk_ref[at, STATE : 2 * STATE] = dot(gaff, in_keys)
        return carry

    lax.fori_loop(0, chunks, chunk, 0)
    wait_all(copies)
    for j in range(2):
        cols = slice(j * half, (j + 1) * half)
        gng_ref[:, cols] = dot(dgate_ref[...], w_ref[cols, :], 1, 1)


def scan_back_kernel(act_ref, step_ref, sig_ref, cum_ref, gcore_ref, gvl_ref, gk_ref, rowq_ref, states_ref,
                     gout_ref, gskip_ref, skip_ref, cext_ref, cw_ref, cb_ref, dl_ref, gconv_ref, head_ref, graw_ref, small_ref,
                     gstate_ref, wide_ref, gact_ref, expand_ref):
    chunks = act_ref.shape[0] // CHUNK
    tiles = INNER // LANES
    fill_expander(expand_ref)
    gstate_ref[...] = gout_ref[...].astype(F32)
    small_ref[...] = jnp.zeros_like(small_ref)
    small_ref[6:7, 0:INNER] = jnp.sum(gskip_ref[...], axis=0, keepdims=True)
    rate = -jnp.exp(dl_ref[0:1, :])
    end = lax.broadcasted_iota(jnp.int32, (CHUNK, LANES), 0) == CHUNK - 1

    def chunk(n, carry):
        gdecay, gbias = carry
        c = chunks - 1 - n
        at = pl.ds(pl.multiple_of(c * CHUNK, CHUNK), CHUNK)
        in_keys = act_ref[at, INNER : INNER + STATE]
        out_keys = act_ref[at, INNER + STATE : CHANNELS]
        cum = cum_ref[at, :]
        step = step_ref[at, :]
        sig = sig_ref[at, :]
        last = cum[CHUNK - 1 : CHUNK]
        small = jnp.concatenate(
            [jnp.exp(cum), jnp.exp(last - cum) * step, jnp.broadcast_to(jnp.exp(last), (8, LANES))], axis=0
        )
        wide_ref[...] = dot(jnp.concatenate(two_parts(small), axis=1), expand_ref[...])
        colq = jnp.zeros((CHUNK, LANES), F32)
        ends = jnp.zeros((8, LANES), F32)
        gin = gk_ref[at, 0:STATE]
        gout = gk_ref[at, STATE : 2 * STATE]
        for tile in range(tiles):
            cols = slice(tile * LANES, (tile + 1) * LANES)
            values = act_ref[at, cols].astype(F32)
            grads = gcore_ref[at, cols].astype(F32)
            gstate = gstate_ref[:, cols]
            gstate_b = gstate.astype(BF16)
            state = states_ref[c, :, cols]
            weight = wide_ref[CHUNK : 2 * CHUNK, cols]
            decay = wide_ref[2 * CHUNK : 2 * CHUNK + 1, cols]
            gvs = weight * dot(in_keys, gstate_b)
            gvalues = gvl_ref[at, cols] + gvs
            colq = colq + head_sums(values * gvalues, tile)
            passed = jnp.sum((values * gvs).reshape(CHUNK // 8, 8, LANES), axis=0) + decay * jnp.sum(
                (gstate * state.astype(F32)).reshape(STATE // 8, 8, LANES), axis=0
            )
            ends = ends + head_sums(passed, tile)
            gin = gin + dot((weight * values).astype(BF16), gstate_b, 1, 1)
            scaled = (wide_ref[0:CHUNK, cols] * grads).astype(BF16)
            gout = gout + dot(scaled, state, 1, 1)
            gstate_ref[:, cols] = decay * gstate + dot(out_keys, scaled, 0, 0)
            gact_ref[:, cols] = gvalues + skip_ref[0:1, cols] * grads
        gact_ref[:, INNER : INNER + STATE] = gin
        gact_ref[:, INNER + STATE : CHANNELS] = gout
        gcum = rowq_ref[at, :] - colq
        gcum = gcum + jnp.where(end, jnp.sum(ends, axis=0, keepdims=True), 0.0)
        glog = running_sum(gcum, reverse=True)
        gdecay = gdecay + jnp.sum((glog * (rate * step)).reshape(CHUNK // 8, 8, LANES), axis=0)
        ratio = jnp.where(step > 0.0, sig / jnp.where(step > 0.0, step, 1.0), 0.0)
        graw = colq * ratio + rate * glog * sig
        gbias = gbias + jnp.sum(graw.reshape(CHUNK // 8, 8, LANES), axis=0)
        first = pl.multiple_of(c * CHUNK, CHUNK)
        graw_ref[at, :] = graw.astype(BF16)
        for tile in range(CHANNELS // LANES):
            cols = slice(tile * LANES, (tile + 1) * LANES)
            part = cext_ref[pl.ds(first, CHUNK + HALO), cols].astype(F32)
            moved = [pltpu.roll(part, KCONV - 1 - k, 0)[HALO:] for k in range(KCONV - 1)] + [part[HALO:]]
            out = cb_ref[0:1, cols]
            for k in range(KCONV):
                out = out + cw_ref[k : k + 1, cols] * moved[k]
            sc = jax.nn.sigmoid(out)
            gconv = gact_ref[:, cols] * (sc * (1.0 + out * (1.0 - sc)))
            gconv_ref[at, cols] = gconv
            for k in range(KCONV):
                small_ref[k : k + 1, cols] = small_ref[k : k + 1, cols] + jnp.sum(
                    gconv * moved[k], axis=0, keepdims=True
                )
            small_ref[4:5, cols] = small_ref[4:5, cols] + jnp.sum(gconv, axis=0, keepdims=True)
        return gdecay, gbias

    zero = jnp.zeros((8, LANES), F32)
    gdecay, gbias = lax.fori_loop(0, chunks, chunk, (zero, zero))
    small_ref[5:6, 0:LANES] = jnp.sum(gdecay, axis=0, keepdims=True)
    small_ref[5:6, LANES : 2 * LANES] = jnp.sum(gbias, axis=0, keepdims=True)
    head_ref[...] = gconv_ref[0:HALO, :]


def conv_back_kernel(rows, devices, scal, gconv_ref, ahead_ref, graw_ref, nh_ref, cw_ref, gproj_ref, keep_ref,
                     send_ref):
    length = gconv_ref.shape[0]
    tall = 4 * HALO
    gproj_ref[:, CHANNELS:] = graw_ref[...]

    def rows_back(first, part_of):
        for tile in range(CHANNELS // LANES):
            cols = slice(tile * LANES, (tile + 1) * LANES)
            part = part_of(cols)
            total = cw_ref[KCONV - 1 : KCONV, cols] * part[:tall]
            for k in range(KCONV - 1):
                ahead = pltpu.roll(part, part.shape[0] - (KCONV - 1 - k), 0)[:tall]
                total = total + cw_ref[k : k + 1, cols] * ahead
            gproj_ref[pl.ds(first, tall), cols] = total.astype(BF16)

    def conv_back(i, carry):
        first = pl.multiple_of(i * tall, tall)
        rows_back(first, lambda cols: gconv_ref[pl.ds(first, tall + 8), cols])
        return carry

    lax.fori_loop(0, length // tall - 1, conv_back, 0)
    rows_back(
        length - tall,
        lambda cols: jnp.concatenate([gconv_ref[length - tall :, cols], ahead_ref[0:8, cols]], axis=0),
    )
    for j in range(WIDTH // 384):
        cols = slice(j * 384, (j + 1) * 384)
        part = dot(nh_ref[HALO:, :], gproj_ref[:, cols], 0, 0).astype(BF16)
        for block in range(devices):
            put_block(
                scal[0], devices, block, keep_ref, send_ref, 0, cols, part[block * rows : (block + 1) * rows]
            )


def token_back_kernel(plan, rows, scal, gproj_ref, gng_ref, x_ref, c_ref, *refs):
    count = PIECES
    pieces = refs[:count]
    gtok_ref, w_ref, acc_ref, sem = refs[count:]
    copies = start_pieces(scal[0], pieces, plan, w_ref, sem, rows)
    length, model = c_ref.shape
    tall = 4 * HALO
    wait_all(copies)
    for j in range(2):
        cols = slice(j * model // 2, (j + 1) * model // 2)
        acc_ref[:, cols] = dot(gproj_ref[...], w_ref[cols, :], 1, 1) + gng_ref[:, cols]
    gain = gain_row(w_ref)

    def norm_back(i, carry):
        at = pl.ds(pl.multiple_of(i * tall, tall), tall)
        u = x_ref[pl.ds(pl.multiple_of(i * tall + HALO, HALO), tall), :].astype(F32)
        scale = lax.rsqrt(jnp.mean(u * u, axis=1, keepdims=True) + EPSILON)
        nh = u * scale
        g = acc_ref[at, :] * gain
        grads = scale * (g - nh * jnp.mean(g * nh, axis=1, keepdims=True))
        gtok_ref[at, :] = (grads + c_ref[at, :].astype(F32)).astype(BF16)
        return carry

    lax.fori_loop(0, length // tall, norm_back, 0)


def call(body, scal, whole, pieces, outs, scratch):
    first = [] if scal is None else [scal]
    smem = pl.BlockSpec(memory_space=pltpu.SMEM)
    vmem = pl.BlockSpec(memory_space=pltpu.VMEM)
    return list(pl.pallas_call(
        body,
        out_shape=[jax.ShapeDtypeStruct(shape, kind) for shape, kind in outs],
        in_specs=[smem] * len(first) + [vmem] * len(whole) + [pl.BlockSpec(memory_space=pl.ANY)] * len(pieces),
        out_specs=[vmem] * len(outs),
        scratch_shapes=scratch,
        compiler_params=pltpu.CompilerParams(vmem_limit_bytes=VMEM_LIMIT),
    )(*first, *whole, *pieces))


def lane_row(vector):
    return jnp.pad(vector, (0, LANES - vector.shape[0]))[None]


def per_device(tokens, lengths, dealing, cotangent, in_weight, out_weight, norm_gain, gate_gain, conv_weight,
               conv_bias, decay_log, step_bias, skip_gain):
    dp, seq = lax.axis_index("dp"), lax.axis_index("seq")
    devices, size = lax.axis_size("dp"), lax.axis_size("seq")
    group = size // 2
    lin = seq * 2 + dp % 2
    holder = lin // group
    place = {"dp": dp, "seq": seq, "micro": holder // 2, "column": holder % 2, "turn": lin % group}
    block_len, model = tokens.shape[2:]
    length = 2 * block_len
    shard_rows = in_weight.shape[0]
    rows = shard_rows * size
    tok = tokens[:, 0]
    cot = cotangent[:, 0]

    gains = jnp.concatenate(
        [norm_gain[:, None], jnp.swapaxes(gate_gain.reshape(2, shard_rows), 0, 1)], axis=1
    )
    conv_shard = jnp.concatenate([in_weight[:, INNER:], gains], axis=1)
    conv_shard = jnp.pad(conv_shard, ((0, 0), (0, WIDTH - conv_shard.shape[1])))
    rest_shard = jnp.concatenate(
        [in_weight[:, :INNER], out_weight[:shard_rows], out_weight[shard_rows:]], axis=1
    )
    masks = spread_masks(devices)
    conv_plan = (masks, [(0, 1, 0, 0, WIDTH)])
    gate_plan = (masks, [(0, 1, 0, 0, model), (rows, 1, 0, model, model)])
    out_plan = (masks, [(0, 2, model, 0, model + LANES)])

    dealt = devices == 8
    if dealt:
        routes = make_routes(place, dp_table(jnp.concatenate([dealing[:, 0], lengths[:, 0]])))
        cot_chain = Chain(cotangent_stages(core_pair(cot, place), routes, place))
        own_length = routes[4, 0]
        moving = [cot_chain]
    else:
        every = lax.all_gather(jnp.concatenate([dealing, lengths], axis=0)[:, 0], "dp", axis=0)
        goals = every[:, :2]
        source_of_out = jnp.argmax(goals == dp, axis=0)
        cot_given = deal_gathered(cot, dealing[:, 0])
        mate = lax.dynamic_index_in_dim(every, dp - dp % 2 + place["column"], 0, keepdims=False)
        own_length = jnp.where(place["micro"] == 0, mate[2], mate[3])
        moving = []

    taps = jnp.pad(conv_weight, ((0, 8 - KCONV), (0, 0)))
    skip_row = jnp.repeat(skip_gain, HDIM)[None]
    n_valid = jnp.clip(own_length - place["turn"] * length, 0, length)
    scal = jnp.stack([dp, n_valid])
    rows_of = (taps, conv_bias[None], lane_row(decay_log), lane_row(step_bias), skip_row, scal)

    shards = Chain(seq_stages(conv_shard, place))
    tok = advance(tok, shards, *moving)
    conv_z = shards.value
    conv = Chain(spread_stages(conv_z.reshape(rows, WIDTH)))
    one, two = to_stretch(tok, place)
    one, two, rows_of, rest_shard = advance((one, two, rows_of, rest_shard), conv, *moving)
    taps, conv_bias_row, decay_row, bias_row, skip_row, scal = rows_of
    first, second = swapped(place["micro"] == 1, (one, two))
    halo = lax.ppermute(second[block_len - HALO :], BOTH, neighbour_pairs(1))
    first, second, halo = advance((first, second, halo), conv, *moving)
    shards = Chain(seq_stages(rest_shard, place))
    while conv.pending is not None:
        halo = advance(halo, conv, *moving)
    x_ext = jnp.concatenate([halo, first, second])
    conv_pieces = conv.value
    gain_rows = jnp.swapaxes(conv_z[:, :, CHANNELS + HEADS + 1 : CHANNELS + HEADS + 3], 1, 2)
    gain_rows = jnp.pad(gain_rows.reshape(2 * rows, 1), ((0, 0), (0, LANES - 1)))
    moving = moving + [shards]
    def sems(plan):
        return pltpu.SemaphoreType.DMA((piece_count(plan),))

    wide = (length, INNER)
    made = call(
        functools.partial(project_kernel, conv_plan, rows),
        scal,
        [x_ext, taps, conv_bias_row, decay_row, bias_row],
        conv_pieces,
        [((length + HALO, model), BF16), ((length + HALO, CHANNELS), BF16), ((length, CHANNELS), BF16)]
        + [((length, LANES), F32)] * 3,
        [pltpu.VMEM((model, WIDTH), BF16), pltpu.VMEM((length + HALO, WIDTH), F32), sems(conv_plan)],
    )
    nh, cext, act, step, sig, cum = advance(made, *moving)
    rest_z = shards.value
    gate_z = [rest_z[:, :, n * model : (n + 1) * model].reshape(rows, model) for n in range(2)]
    out_z = jnp.concatenate([rest_z[:, :, INNER : INNER + model], rest_z[:, :, INNER + model :]], axis=1)
    out_z = out_z.reshape(2 * rows, model)
    rest = Chain(spread_stages(jnp.concatenate([jnp.concatenate(gate_z), out_z, gain_rows], axis=1)))
    moving[-1] = rest
    local, update, total = advance(
        call(
            local_kernel,
            None,
            [act, step, cum],
            [],
            [(wide, F32), ((STATE, INNER), BF16), ((8, LANES), F32)],
            [pltpu.VMEM((STATE, INNER), F32), pltpu.VMEM((2 * LANES, INNER), BF16)],
        ),
        *moving,
    )
    passing = jnp.repeat(jnp.exp(total[0, :HEADS]), HDIM)[None] if group > 2 else None

    def relay(own, pairs):
        carried = None
        for _ in range(group - 1):
            given = own if carried is None else (passing * carried.astype(F32) + own.astype(F32)).astype(BF16)
            carried = lax.ppermute(given, BOTH, pairs)
        return jnp.zeros_like(own) if carried is None else carried

    state_in = relay(update, neighbour_pairs(1))
    while rest.pending is not None:
        state_in = advance(state_in, *moving)
    if dealt:
        while cot_chain.pending is not None:
            advance((), cot_chain)
        c_own = cot_chain.value
    else:
        c_own = jnp.concatenate(swapped(place["micro"] == 1, to_stretch(cot_given, place)))
    rest_pieces = rest.value

    out, gn, dgate, gcore, rowq, lsg, states, gskip = call(
        functools.partial(middle_kernel, gate_plan, out_plan, rows),
        scal,
        [local, act, step, cum, nh, state_in, x_ext, c_own, skip_row],
        rest_pieces,
        [((length, model), BF16), (wide, BF16), (wide, BF16), (wide, BF16), ((length, LANES), F32),
         ((STATE, INNER), BF16), ((length // CHUNK, STATE, INNER), BF16), ((8, INNER), F32)],
        [pltpu.VMEM((INNER, model + LANES), BF16), pltpu.VMEM((model, INNER), BF16), pltpu.VMEM(wide, F32),
         pltpu.VMEM((8, INNER), F32), pltpu.VMEM((length, model), BF16), pltpu.VMEM(wide, F32),
         pltpu.VMEM((STATE, INNER), F32), pltpu.VMEM((3 * CHUNK + 8, INNER), F32),
         pltpu.VMEM((CHUNK, INNER), F32), pltpu.VMEM((CHUNK, INNER), F32), pltpu.VMEM((STATE, INNER), F32),
         pltpu.VMEM((2 * LANES, INNER), BF16), sems(gate_plan), sems(out_plan)],
    )
    if dealt:
        moving = [Chain(output_stages(out, routes, place))]
        out_chain = moving[0]
    else:
        moving = []
        blocks = jnp.stack(swapped(place["seq"] % 2 == 1, from_stretch(out[:block_len], out[block_len:], place)))
        outputs = deal_gathered(blocks, source_of_out)
    grad_out_state = relay(lsg, neighbour_pairs(-1))

    half_dp = devices // 2
    keep1, send1, gcore, dgate = advance(
        call(
            functools.partial(early_kernel, rows, devices),
            scal,
            [gn, c_own, nh, dgate],
            [],
            [((half_dp, 4 * rows, model), BF16)] * 2,
            [pltpu.VMEM((length, model), BF16)],
        )
        + [gcore, dgate],
        *moving,
    )

    def early_take(part, index):
        gates = part[: 2 * rows].reshape(2, size, shard_rows, model)
        gates = lax.dynamic_index_in_dim(gates, index, 1, keepdims=False).reshape(2 * shard_rows, model)
        outs = part[2 * rows :].reshape(size, 2 * shard_rows, model)
        return jnp.concatenate([gates, lax.dynamic_index_in_dim(outs, index, 0, keepdims=False)])

    early = Chain(reduce_stages(keep1, send1, place, early_take))
    moving.append(early)
    made = call(
        functools.partial(local_back_kernel, gate_plan, rows),
        scal,
        [act, step, cum, gcore, dgate],
        rest_pieces,
        [(wide, F32), ((length, 2 * STATE), F32), ((length, model), F32)],
        [pltpu.VMEM((model, INNER), BF16), sems(gate_plan)],
    )
    gvl, gk, gng, grad_out_state = advance(made + [grad_out_state], *moving)
    gconv, head, graw, small = advance(
        call(
            scan_back_kernel,
            None,
            [act, step, sig, cum, gcore, gvl, gk, rowq, states, grad_out_state, gskip, skip_row, cext, taps,
             conv_bias_row, decay_row],
            [],
            [((length, CHANNELS), F32), ((HALO, CHANNELS), F32), ((length, LANES), BF16), ((8, WIDTH), F32)],
            [pltpu.VMEM((STATE, INNER), F32), pltpu.VMEM((2 * CHUNK + 8, INNER), F32),
             pltpu.VMEM((CHUNK, CHANNELS), F32), pltpu.VMEM((2 * LANES, INNER), BF16)],
        ),
        *moving,
    )
    ahead = lax.ppermute(head, BOTH, neighbour_pairs(-1))
    sums = Chain(sum_stages(small))
    moving.append(sums)
    gproj, keep2, send2 = advance(
        call(
            functools.partial(conv_back_kernel, rows, devices),
            scal,
            [gconv, ahead, graw, nh, taps],
            [],
            [((length, WIDTH), BF16)] + [((half_dp, rows, WIDTH), BF16)] * 2,
            [],
        ),
        *moving,
    )

    def late_take(part, index):
        return lax.dynamic_index_in_dim(part.reshape(size, shard_rows, WIDTH), index, 0, keepdims=False)

    final = Chain(reduce_stages(keep2, send2, place, late_take))
    moving.append(final)
    (gtok,) = advance(
        call(
            functools.partial(token_back_kernel, conv_plan, rows),
            scal,
            [gproj, gng, x_ext, c_own],
            conv_pieces,
            [((length, model), BF16)],
            [pltpu.VMEM((model, WIDTH), BF16), pltpu.VMEM((length, model), F32), sems(conv_plan)],
        ),
        *moving,
    )

    one, two = from_stretch(gtok[:block_len], gtok[block_len:], place)
    one = advance(one, *moving)
    back = one, advance(two, *moving)
    while any(chain.pending is not None for chain in moving):
        advance((), *moving)
    grad_tokens = jnp.stack(swapped(place["seq"] % 2 == 1, back))
    if dealt:
        outputs = out_chain.value

    early_sum, late_sum, sums = early.value, final.value, sums.value
    raw_in = jnp.concatenate(
        [early_sum[:shard_rows], early_sum[shard_rows : 2 * shard_rows],
         late_sum[:, : in_weight.shape[1] - INNER]], axis=1
    )
    raw_out = early_sum[2 * shard_rows :]
    grad_norm_gain = jnp.sum(raw_in * in_weight.astype(F32), axis=1) / norm_gain.astype(F32)
    grad_gate_gain = jnp.sum(raw_out * out_weight.astype(F32), axis=1) / gate_gain.astype(F32)
    grad_skip = jnp.sum(sums[6, :INNER].reshape(HEADS, HDIM), axis=1)
    return (
        outputs[:, None],
        grad_tokens[:, None],
        raw_in,
        raw_out,
        grad_norm_gain,
        grad_gate_gain,
        sums[0:KCONV, :CHANNELS],
        sums[4, :CHANNELS],
        sums[5, :HEADS],
        sums[5, LANES : LANES + HEADS],
        grad_skip,
    )


def solution(mesh):
    in_specs = (
        P(None, "dp", "seq", None),
        P(None, "dp"),
        P(None, "dp"),
        P(None, "dp", "seq", None),
        P(BOTH, None),
        P(BOTH, None),
        P(BOTH),
        P(BOTH),
        P(),
        P(),
        P(),
        P(),
        P(),
    )
    out_specs = (
        P(None, "dp", "seq", None),
        P(None, "dp", "seq", None),
        P(BOTH, None),
        P(BOTH, None),
        P(BOTH),
        P(BOTH),
        P(),
        P(),
        P(),
        P(),
        P(),
    )
    return jax.shard_map(per_device, mesh=mesh, in_specs=in_specs, out_specs=out_specs, check_vma=False)
```

profile of v0, /device:TPU:0, one launch (start us, length us, event | category | flops | bytes accessed | tf_op | source)
XLA Modules:
  0.0 294.2 jit_solution(10376809143515709853)
XLA Ops:
  3.4 3.1 %collective-permute-start = (bf16[24,1920]{1,0:T(8,128)(2,1)S(1)}, bf16[24,1920]{1,0:T(8,128)(2,1)S(1)}, u32[]{:S(2)}, u32[]{:S(2)}) collective-permute-start(bf16[24,1920]{1,0:T(8,128)(2,1)S(1)} %pad.19), channel_id=1, source_target_pairs={{0,1},{1,2},{2,3},{3,0},{4,5},{5,6},{6,7},{7,4},{8,9},{9,10},{10,1... | collective-permute-start | bytes 276488 | tf_op jit(solution)/shard_map/ppermute | solution.py:46
  6.5 2.6 collective-permute-start.1
  18.8 3.3 %collective-permute-start.5 = (bf16[256,768]{1,0:T(8,128)(2,1)S(1)}, bf16[256,768]{1,0:T(8,128)(2,1)S(1)}, u32[]{:S(2)}, u32[]{:S(2)}) collective-permute-start(bf16[256,768]{1,0:T(8,128)(2,1)S(1)} %get-tuple-element.299), channel_id=1, source_target_pairs={{0,2},{1,0},{2,6},{3,4},{4,3},{5,1},{6,7},{7,5},{8,10},{9,8},{10,1... | collective-permute-start | bytes 1179656 | tf_op jit(solution)/shard_map/ppermute | solution.py:83
  23.7 8.1 %collective-permute-done.7 = s32[2,4]{1,0:T(2,128)S(1)} collective-permute-done((s32[2,4]{1,0:T(2,128)S(1)}, s32[2,4]{1,0:T(2,128)S(1)}, u32[]{:S(2)}, u32[]{:S(2)}) %collective-permute-start.7) | collective-permute-done | bytes 64 | tf_op jit(solution)/shard_map/ppermute | solution.py:30
  61.9 13.4 %shard_map.214 = (bf16[528,768]{1,0:T(8,128)(2,1)}, bf16[528,1792]{1,0:T(8,128)(2,1)}, bf16[512,1792]{1,0:T(8,128)(2,1)}, f32[512,128]{1,0:T(8,128)}, f32[512,128]{1,0:T(8,128)}, /*index=5*/f32[512,128]{1,0:T(8,128)}) custom-call(s32[2]{0:T(128)} %pad_add_fusion.4.scal, bf16[528,768]{1,0:T(8,128)(2,1)} %copy-done.1, f32[8,1792]{1,0:T(8,128)} %pad.20.cw_ref, ...), custom_call_target="tpu_custom_call" | custom-call | tf_op jit(solution)/shard_map/pallas_call | solution.py:921
  75.4 2.7 shard_map.216
  81.8 7.6 %shard_map.215 = (f32[512,1536]{1,0:T(8,128)}, bf16[128,1536]{1,0:T(8,128)(2,1)}, f32[8,128]{1,0:T(8,128)}) custom-call(bf16[512,1792]{1,0:T(8,128)(2,1)} %get-tuple-element.156.act_ref, f32[512,128]{1,0:T(8,128)} %get-tuple-element.157.step_ref, f32[512,128]{1,0:T(8,128)} %get-tuple-element.159.cum_ref), custom_call_target="tpu_custom_call" | custom-call | tf_op jit(solution)/shard_map/pallas_call | solution.py:921
  91.1 4.7 %collective-permute-start.25 = (bf16[2,192,1664]{2,1,0:T(8,128)(2,1)S(1)}, bf16[2,192,1664]{2,1,0:T(8,128)(2,1)S(1)}, u32[]{:S(2)}, u32[]{:S(2)}) collective-permute-start(bf16[2,192,1664]{2,1,0:T(8,128)(2,1)S(1)} %pad_maximum_fusion.refs_0_), channel_id=1, source_target_pairs={{0,4},{4,0},{8,12},{12,8},{16,20},{20,16},{24,28},{28,24},{1,5},{5... | collective-permute-start | bytes 3833864 | tf_op jit(solution)/shard_map/ppermute | solution.py:30
  97.1 3.1 %collective-permute-start.22 = (bf16[128,1536]{1,0:T(8,128)(2,1)S(1)}, bf16[128,1536]{1,0:T(8,128)(2,1)S(1)}, u32[]{:S(2)}, u32[]{:S(2)}) collective-permute-start(bf16[128,1536]{1,0:T(8,128)(2,1)S(1)} %copy-done.46), channel_id=1, source_target_pairs={{0,4},{1,5},{2,6},{3,7},{8,12},{9,13},{10,14},{11,15},{16,20},{17,... | collective-permute-start | bytes 1179656 | tf_op jit(solution)/shard_map/ppermute | solution.py:1039
  100.2 6.2 %collective-permute-done.23 = bf16[256,768]{1,0:T(8,128)(2,1)S(1)} collective-permute-done((bf16[256,768]{1,0:T(8,128)(2,1)S(1)}, bf16[256,768]{1,0:T(8,128)(2,1)S(1)}, u32[]{:S(2)}, u32[]{:S(2)}) %collective-permute-start.23) | collective-permute-done | bytes 393248 | tf_op jit(solution)/shard_map/ppermute | solution.py:83
  107.3 3.4 %collective-permute-start.26 = (bf16[2,192,1664]{2,1,0:T(8,128)(2,1)S(1)}, bf16[2,192,1664]{2,1,0:T(8,128)(2,1)}, u32[]{:S(2)}, u32[]{:S(2)}) collective-permute-start(bf16[2,192,1664]{2,1,0:T(8,128)(2,1)S(1)} %collective-permute-done.24.refs_1_), channel_id=1, source_target_pairs={{0,4},{4,0},{8,12},{12,8},{16,20},{20,16},{24,28},{28,24},{1,5},{5... | collective-permute-start | bytes 3833864 | tf_op jit(solution)/shard_map/ppermute | solution.py:30
  113.5 25.5 %shard_map.217 = (bf16[512,768]{1,0:T(8,128)(2,1)}, bf16[512,1536]{1,0:T(8,128)(2,1)}, bf16[512,1536]{1,0:T(8,128)(2,1)}, bf16[512,1536]{1,0:T(8,128)(2,1)}, f32...) custom-call(s32[2]{0:T(128)} %pad_add_fusion.4.scal, ...), custom_call_target="tpu_custom_call" | custom-call | tf_op jit(solution)/shard_map/pallas_call | solution.py:921
  140.8 10.6 %shard_map.218 = (bf16[4,384,768]{2,1,0:T(8,128)(2,1)}, bf16[4,384,768]{2,1,0:T(8,128)(2,1)}) custom-call(s32[2]{0:T(128)} %pad_add_fusion.4.scal, bf16[512,1536]{1,0:T(8,128)(2,1)} %get-tuple-element.180.gn_ref, bf16[512,768]{1,0:T(8,128)(2,1)} %pad_maximum_fusion.2.c_ref, bf16[528,768]{1,0:T(8,128)(2,1)} %get-tuple-element.169.nh_ref, ...), custom_call_target="tpu_custom_call" | custom-call | tf_op jit(solution)/shard_map/pallas_call | solution.py:921
  151.4 4.9 %collective-permute-start.30 = (bf16[4,384,768]{2,1,0:T(8,128)(2,1)}, bf16[4,384,768]{2,1,0:T(8,128)(2,1)S(1)}, u32[]{:S(2)}, u32[]{:S(2)}) collective-permute-start(bf16[4,384,768]{2,1,0:T(8,128)(2,1)} %get-tuple-element.192), channel_id=1, source_target_pairs={{0,4},{4,0},{8,12},{12,8},{16,20},{20,16},{24,28},{28,24},{1,5},{5... | collective-permute-start | bytes 7077896 | tf_op jit(solution)/shard_map/ppermute | solution.py:30
  158.1 12.3 %shard_map.219 = (f32[512,1536]{1,0:T(8,128)}, f32[512,256]{1,0:T(8,128)}, f32[512,768]{1,0:T(8,128)}) custom-call(s32[2]{0:T(128)} %pad_add_fusion.4.scal, bf16[512,1792]{1,0:T(8,128)(2,1)} %get-tuple-element.156.act_ref, f32[512,128]{1,0:T(8,128)} %get-tuple-element.157.step_ref, f32[512,128]{1,0:T(8,128)} %get-tuple-element.159.cum_ref, ...), custom_call_target="tpu_custom_call" | custom-call | tf_op jit(solution)/shard_map/pallas_call | solution.py:921
  177.7 19.0 %shard_map.220 = (f32[512,1792]{1,0:T(8,128)}, f32[16,1792]{1,0:T(8,128)}, bf16[512,128]{1,0:T(8,128)(2,1)}, f32[8,1920]{1,0:T(8,128)}) custom-call(bf16[512,1792]{1,0:T(8,128)(2,1)} %get-tuple-element.156.act_ref, f32[512,128]{1,0:T(8,128)} %get-tuple-element.157.step_ref, f32[512,128]{1,0:T(8,128)} %get-tuple-element.158.sig_ref, ...), custom_call_target="tpu_custom_call" | custom-call | tf_op jit(solution)/shard_map/pallas_call | solution.py:921
  209.3 10.3 %shard_map.221 = (bf16[512,1920]{1,0:T(8,128)(2,1)}, bf16[4,96,1920]{2,1,0:T(8,128)(2,1)}, bf16[4,96,1920]{2,1,0:T(8,128)(2,1)}) custom-call(s32[2]{0:T(128)} %pad_add_fusion.4.scal, f32[512,1792]{1,0:T(8,128)} %get-tuple-element.208.gconv_ref, f32[16,1792]{1,0:T(8,128)} %copy-done.38, bf16[512,128]{1,0:T(8,128)(2,1)} %get-tuple-element.210.graw_ref, ...), custom_call_target="tpu_custom_call" | custom-call | tf_op jit(solution)/shard_map/pallas_call | solution.py:921
  223.0 3.3 %collective-permute-start.42 = (f32[8,1920]{1,0:T(8,128)S(1)}, f32[8,1920]{1,0:T(8,128)}, u32[]{:S(2)}, u32[]{:S(2)}) collective-permute-start(f32[8,1920]{1,0:T(8,128)S(1)} %add.376), channel_id=1, source_target_pairs={{0,2},{1,3},{2,0},{3,1},{4,6},{5,7},{6,4},{7,5},{8,10},{9,11},{10,... | collective-permute-start | bytes 184328 | tf_op jit(solution)/shard_map/ppermute | solution.py:197
  235.8 9.2 %shard_map.222 = bf16[512,768]{1,0:T(8,128)(2,1)} custom-call(s32[2]{0:T(128)} %pad_add_fusion.4.scal, bf16[512,1920]{1,0:T(8,128)(2,1)} %get-tuple-element.217.gproj_ref, f32[512,768]{1,0:T(8,128)} %get-tuple-element.218.gng_ref, bf16[528,768]{1,0:T(8,128)(2,1)} %copy-done.1, bf16[512,768]{1,0:T(8,128)(2,1)} %pad_maximum_fusion.2.c_ref, ...), custom_call_target="tpu_custom_call" | custom-call | tf_op jit(solution)/shard_map/pallas_call | solution.py:921
  245.0 3.5 %collective-permute-done.40 = bf16[96,768]{1,0:T(8,128)(2,1)S(1)} collective-permute-done((bf16[96,768]{1,0:T(8,128)(2,1)}, bf16[96,768]{1,0:T(8,128)(2,1)S(1)}, u32[]{:S(2)}, u32[]{:S(2)}) %collective-permute-start.40) | collective-permute-done | bytes 147488 | tf_op jit(solution)/shard_map/ppermute | solution.py:46
  256.3 2.7 shard_map.224
  259.8 3.4 %collective-permute-start.48 = (bf16[256,768]{1,0:T(8,128)(2,1)S(1)}, bf16[256,768]{1,0:T(8,128)(2,1)S(1)}, u32[]{:S(2)}, u32[]{:S(2)}) collective-permute-start(bf16[256,768]{1,0:T(8,128)(2,1)S(1)} %get-tuple-element.281), channel_id=1, source_target_pairs={{2,0},{0,1},{6,2},{4,3},{3,4},{1,5},{7,6},{5,7},{10,8},{8,9},{14,1... | collective-permute-start | bytes 1179656 | tf_op jit(solution)/shard_map/ppermute | solution.py:94
  272.2 8.3 %collective-permute-done.48 = bf16[256,768]{1,0:T(8,128)(2,1)S(1)} collective-permute-done((bf16[256,768]{1,0:T(8,128)(2,1)S(1)}, bf16[256,768]{1,0:T(8,128)(2,1)S(1)}, u32[]{:S(2)}, u32[]{:S(2)}) %collective-permute-start.48) | collective-permute-done | bytes 393248 | tf_op jit(solution)/shard_map/ppermute | solution.py:94
  285.3 2.8 collective-permute-start.53
  (298 shorter events, 118.0 us)
Async XLA Ops:
  15.7 24.5 %collective-permute-start.10 = (bf16[2,2,128,768]{3,2,0,1:T(8,128)(2,1)S(1)}, bf16[2,2,128,768]{3,2,0,1:T(8,128)(2,1)}, u32[]{:S(2)}, u32[]{:S(2)}) collective-permute-start(bf16[2,2,128,768]{3,2,0,1:T(8,128)(2,1)S(1)} %pad_maximum_fusion.1), channel_id=1, source_target_pairs={{0,8},{4,20},{8,0},{12,28},{16,24},{20,4},{24,16},{28,12},{1,9},{5... | collective-permute-start | bytes 2359304 | tf_op jit(solution)/shard_map/ppermute | solution.py:41
  17.5 22.7 %collective-permute-start.9 = (bf16[1,96,1920]{2,1,0:T(8,128)(2,1)S(1)}, bf16[1,96,1920]{2,1,0:T(8,128)(2,1)}, u32[]{:S(2)}, u32[]{:S(2)}) collective-permute-start(bf16[1,96,1920]{2,1,0:T(8,128)(2,1)S(1)} %bitcast.150), channel_id=1, source_target_pairs={{0,8},{4,20},{8,0},{12,28},{16,24},{20,4},{24,16},{28,12},{1,9},{5... | collective-permute-start | bytes 1105928 | tf_op jit(solution)/shard_map/ppermute | solution.py:41
  18.1 22.1 %collective-permute-start.4 = (bf16[256,768]{1,0:T(8,128)(2,1)S(1)}, bf16[256,768]{1,0:T(8,128)(2,1)S(1)}, u32[]{:S(2)}, u32[]{:S(2)}) collective-permute-start(bf16[256,768]{1,0:T(8,128)(2,1)S(1)} %get-tuple-element.300), channel_id=1, source_target_pairs={{0,0},{1,2},{2,4},{3,6},{4,1},{5,3},{6,5},{7,7},{8,8},{9,10},{10,1... | collective-permute-start | bytes 1179656 | tf_op jit(solution)/shard_map/ppermute | solution.py:82
  18.8 21.4 %collective-permute-start.5 = (bf16[256,768]{1,0:T(8,128)(2,1)S(1)}, bf16[256,768]{1,0:T(8,128)(2,1)S(1)}, u32[]{:S(2)}, u32[]{:S(2)}) collective-permute-start(bf16[256,768]{1,0:T(8,128)(2,1)S(1)} %get-tuple-element.299), channel_id=1, source_target_pairs={{0,2},{1,0},{2,6},{3,4},{4,3},{5,1},{6,7},{7,5},{8,10},{9,8},{10,1... | collective-permute-start | bytes 1179656 | tf_op jit(solution)/shard_map/ppermute | solution.py:83
  53.7 21.7 %collective-permute-start.15 = (bf16[2,2,128,768]{3,2,1,0:T(8,128)(2,1)}, bf16[2,2,128,768]{3,2,1,0:T(8,128)(2,1)}, u32[]{:S(2)}, u32[]{:S(2)}) collective-permute-start(bf16[2,2,128,768]{3,2,1,0:T(8,128)(2,1)} %shard_map.213), channel_id=1, source_target_pairs={{0,16},{4,12},{8,24},{12,4},{16,0},{20,28},{24,8},{28,20},{1,17},{... | collective-permute-start | bytes 2359304 | tf_op jit(solution)/shard_map/ppermute | solution.py:41
  55.6 19.8 %collective-permute-start.16 = (bf16[24,3072]{1,0:T(8,128)(2,1)}, bf16[24,3072]{1,0:T(8,128)(2,1)S(1)}, u32[]{:S(2)}, u32[]{:S(2)}) collective-permute-start(bf16[24,3072]{1,0:T(8,128)(2,1)} %pad_maximum_fusion.11), channel_id=1, source_target_pairs={{0,1},{1,2},{2,3},{3,0},{4,5},{5,6},{6,7},{7,4},{8,9},{9,10},{10,1... | collective-permute-start | bytes 442376 | tf_op jit(solution)/shard_map/ppermute | solution.py:46
  57.6 17.7 %collective-permute-start.17 = (bf16[24,3072]{1,0:T(8,128)(2,1)}, bf16[24,3072]{1,0:T(8,128)(2,1)S(1)}, u32[]{:S(2)}, u32[]{:S(2)}) collective-permute-start(bf16[24,3072]{1,0:T(8,128)(2,1)} %pad_maximum_fusion.11), channel_id=1, source_target_pairs={{0,2},{1,3},{2,0},{3,1},{4,6},{5,7},{6,4},{7,5},{8,10},{9,11},{10,... | collective-permute-start | bytes 442376 | tf_op jit(solution)/shard_map/ppermute | solution.py:46
  59.3 16.0 %collective-permute-start.18 = (bf16[24,3072]{1,0:T(8,128)(2,1)}, bf16[24,3072]{1,0:T(8,128)(2,1)}, u32[]{:S(2)}, u32[]{:S(2)}) collective-permute-start(bf16[24,3072]{1,0:T(8,128)(2,1)} %pad_maximum_fusion.11), channel_id=1, source_target_pairs={{0,3},{1,0},{2,1},{3,2},{4,7},{5,4},{6,5},{7,6},{8,11},{9,8},{10,9... | collective-permute-start | bytes 442376 | tf_op jit(solution)/shard_map/ppermute | solution.py:46
  89.9 17.3 %collective-permute-start.24 = (bf16[2,192,1664]{2,1,0:T(8,128)(2,1)S(1)}, bf16[2,192,1664]{2,1,0:T(8,128)(2,1)S(1)}, u32[]{:S(2)}, u32[]{:S(2)}) collective-permute-start(bf16[2,192,1664]{2,1,0:T(8,128)(2,1)S(1)} %pad_maximum_fusion.refs_0_), channel_id=1, source_target_pairs={{0,16},{4,12},{8,24},{12,4},{16,0},{20,28},{24,8},{28,20},{1,17},{... | collective-permute-start | bytes 3833864 | tf_op jit(solution)/shard_map/ppermute | solution.py:41
  91.1 16.2 %collective-permute-start.25 = (bf16[2,192,1664]{2,1,0:T(8,128)(2,1)S(1)}, bf16[2,192,1664]{2,1,0:T(8,128)(2,1)S(1)}, u32[]{:S(2)}, u32[]{:S(2)}) collective-permute-start(bf16[2,192,1664]{2,1,0:T(8,128)(2,1)S(1)} %pad_maximum_fusion.refs_0_), channel_id=1, source_target_pairs={{0,4},{4,0},{8,12},{12,8},{16,20},{20,16},{24,28},{28,24},{1,5},{5... | collective-permute-start | bytes 3833864 | tf_op jit(solution)/shard_map/ppermute | solution.py:30
  151.4 19.0 %collective-permute-start.30 = (bf16[4,384,768]{2,1,0:T(8,128)(2,1)}, bf16[4,384,768]{2,1,0:T(8,128)(2,1)S(1)}, u32[]{:S(2)}, u32[]{:S(2)}) collective-permute-start(bf16[4,384,768]{2,1,0:T(8,128)(2,1)} %get-tuple-element.192), channel_id=1, source_target_pairs={{0,4},{4,0},{8,12},{12,8},{16,20},{20,16},{24,28},{28,24},{1,5},{5... | collective-permute-start | bytes 7077896 | tf_op jit(solution)/shard_map/ppermute | solution.py:30
  156.3 14.1 %collective-permute-start.29 = (bf16[256,768]{1,0:T(8,128)(2,1)S(1)}, bf16[256,768]{1,0:T(8,128)(2,1)S(1)}, u32[]{:S(2)}, u32[]{:S(2)}) collective-permute-start(bf16[256,768]{1,0:T(8,128)(2,1)S(1)} %get-tuple-element.289), channel_id=1, source_target_pairs={{2,0},{0,1},{6,2},{4,3},{3,4},{1,5},{7,6},{5,7},{10,8},{8,9},{14,1... | collective-permute-start | bytes 1179656 | tf_op jit(solution)/shard_map/ppermute | solution.py:94
  156.6 13.8 %collective-permute-start.28 = (bf16[128,1536]{1,0:T(8,128)(2,1)}, bf16[128,1536]{1,0:T(8,128)(2,1)}, u32[]{:S(2)}, u32[]{:S(2)}) collective-permute-start(bf16[128,1536]{1,0:T(8,128)(2,1)} %get-tuple-element.191), channel_id=1, source_target_pairs={{4,0},{5,1},{6,2},{7,3},{12,8},{13,9},{14,10},{15,11},{20,16},{21,... | collective-permute-start | bytes 1179656 | tf_op jit(solution)/shard_map/ppermute | solution.py:1039
  173.0 23.7 %collective-permute-start.32 = (bf16[2,384,768]{2,1,0:T(8,128)(2,1)}, bf16[2,384,768]{2,1,0:T(8,128)(2,1)}, u32[]{:S(2)}, u32[]{:S(2)}) collective-permute-start(bf16[2,384,768]{2,1,0:T(8,128)(2,1)} %add_convert_fusion), channel_id=1, source_target_pairs={{0,8},{4,20},{8,0},{12,28},{16,24},{20,4},{24,16},{28,12},{1,9},{5... | collective-permute-start | bytes 3538952 | tf_op jit(solution)/shard_map/ppermute | solution.py:41
  174.7 22.0 %collective-permute-start.31 = (bf16[2,128,768]{2,1,0:T(8,128)(2,1)S(1)}, bf16[2,128,768]{2,1,0:T(8,128)(2,1)S(1)}, u32[]{:S(2)}, u32[]{:S(2)}) collective-permute-start(bf16[2,128,768]{2,1,0:T(8,128)(2,1)S(1)} %get-tuple-element.286), channel_id=1, source_target_pairs={{0,4},{4,0},{8,12},{12,8},{16,20},{20,16},{24,28},{28,24},{1,5},{5... | collective-permute-start | bytes 1179656 | tf_op jit(solution)/shard_map/ppermute | solution.py:30
  198.6 21.0 %collective-permute-start.34 = (bf16[2,2,128,768]{3,2,1,0:T(8,128)(2,1)S(1)}, bf16[2,2,128,768]{3,2,1,0:T(8,128)(2,1)S(1)}, u32[]{:S(2)}, u32[]{:S(2)}) collective-permute-start(bf16[2,2,128,768]{3,2,1,0:T(8,128)(2,1)S(1)} %pad_maximum_fusion.3.pair_ref), channel_id=1, source_target_pairs={{0,8},{4,20},{8,0},{12,28},{16,24},{20,4},{24,16},{28,12},{1,9},{5... | collective-permute-start | bytes 2359304 | tf_op jit(solution)/shard_map/ppermute | solution.py:41
  201.8 17.8 %collective-permute-start.35 = (bf16[384,768]{1,0:T(8,128)(2,1)}, bf16[384,768]{1,0:T(8,128)(2,1)}, u32[]{:S(2)}, u32[]{:S(2)}) collective-permute-start(bf16[384,768]{1,0:T(8,128)(2,1)} %fusion.3), channel_id=1, source_target_pairs={{0,16},{4,12},{8,24},{12,4},{16,0},{20,28},{24,8},{28,20},{1,17},{... | collective-permute-start | bytes 1769480 | tf_op jit(solution)/shard_map/ppermute | solution.py:41
  219.6 28.9 %collective-permute-start.43 = (bf16[4,96,1920]{2,1,0:T(8,128)(2,1)}, bf16[4,96,1920]{2,1,0:T(8,128)(2,1)}, u32[]{:S(2)}, u32[]{:S(2)}) collective-permute-start(bf16[4,96,1920]{2,1,0:T(8,128)(2,1)} %get-tuple-element.222), channel_id=1, source_target_pairs={{0,4},{4,0},{8,12},{12,8},{16,20},{20,16},{24,28},{28,24},{1,5},{5... | collective-permute-start | bytes 4423688 | tf_op jit(solution)/shard_map/ppermute | solution.py:30
  228.7 19.9 %collective-permute-start.38 = (bf16[2,2,128,768]{3,2,1,0:T(8,128)(2,1)}, bf16[2,2,128,768]{3,2,1,0:T(8,128)(2,1)S(1)}, u32[]{:S(2)}, u32[]{:S(2)}) collective-permute-start(bf16[2,2,128,768]{3,2,1,0:T(8,128)(2,1)} %shard_map.223), channel_id=1, source_target_pairs={{0,16},{4,12},{8,24},{12,4},{16,0},{20,28},{24,8},{28,20},{1,17},{... | collective-permute-start | bytes 2359304 | tf_op jit(solution)/shard_map/ppermute | solution.py:41
  233.9 14.7 %collective-permute-start.40 = (bf16[96,768]{1,0:T(8,128)(2,1)}, bf16[96,768]{1,0:T(8,128)(2,1)S(1)}, u32[]{:S(2)}, u32[]{:S(2)}) collective-permute-start(bf16[96,768]{1,0:T(8,128)(2,1)} %add_convert_fusion.5), channel_id=1, source_target_pairs={{0,2},{1,3},{2,0},{3,1},{4,6},{5,7},{6,4},{7,5},{8,10},{9,11},{10,... | collective-permute-start | bytes 442376 | tf_op jit(solution)/shard_map/ppermute | solution.py:46
  235.7 12.9 %collective-permute-start.39 = (bf16[96,768]{1,0:T(8,128)(2,1)S(1)}, bf16[96,768]{1,0:T(8,128)(2,1)S(1)}, u32[]{:S(2)}, u32[]{:S(2)}) collective-permute-start(bf16[96,768]{1,0:T(8,128)(2,1)S(1)} %add_convert_fusion.6), channel_id=1, source_target_pairs={{0,1},{1,2},{2,3},{3,0},{4,5},{5,6},{6,7},{7,4},{8,9},{9,10},{10,1... | collective-permute-start | bytes 442376 | tf_op jit(solution)/shard_map/ppermute | solution.py:46
  252.8 13.2 %collective-permute-start.47 = (bf16[2,96,1920]{2,1,0:T(8,128)(2,1)}, bf16[2,96,1920]{2,1,0:T(8,128)(2,1)}, u32[]{:S(2)}, u32[]{:S(2)}) collective-permute-start(bf16[2,96,1920]{2,1,0:T(8,128)(2,1)} %add_convert_fusion.1), channel_id=1, source_target_pairs={{0,8},{4,20},{8,0},{12,28},{16,24},{20,4},{24,16},{28,12},{1,9},{5... | collective-permute-start | bytes 2211848 | tf_op jit(solution)/shard_map/ppermute | solution.py:41
  259.8 20.8 %collective-permute-start.48 = (bf16[256,768]{1,0:T(8,128)(2,1)S(1)}, bf16[256,768]{1,0:T(8,128)(2,1)S(1)}, u32[]{:S(2)}, u32[]{:S(2)}) collective-permute-start(bf16[256,768]{1,0:T(8,128)(2,1)S(1)} %get-tuple-element.281), channel_id=1, source_target_pairs={{2,0},{0,1},{6,2},{4,3},{3,4},{1,5},{7,6},{5,7},{10,8},{8,9},{14,1... | collective-permute-start | bytes 1179656 | tf_op jit(solution)/shard_map/ppermute | solution.py:94
  267.2 13.4 %collective-permute-start.50 = (bf16[96,1920]{1,0:T(8,128)(2,1)S(1)}, bf16[96,1920]{1,0:T(8,128)(2,1)S(1)}, u32[]{:S(2)}, u32[]{:S(2)}) collective-permute-start(bf16[96,1920]{1,0:T(8,128)(2,1)S(1)} %fusion.6), channel_id=1, source_target_pairs={{0,16},{4,12},{8,24},{12,4},{16,0},{20,28},{24,8},{28,20},{1,17},{... | collective-permute-start | bytes 1105928 | tf_op jit(solution)/shard_map/ppermute | solution.py:41
  (82 other events, 581.4 us)
where the time goes:
time: 296 us; the launch traced here: 294 us
  Pallas kernels  120 us (41%)
  starting transfers between devices  76.2 us (26%)
  waiting for transfers between devices  35.5 us (12%)
  other arithmetic  31.2 us (11%)
  local copies, waits for them, and re-layouts  29.2 us (10%)
    pallas_call x8, Pallas kernels, call(): pl.pallas_call(body, out_shape=[jax.ShapeDtypeStruct(shape, kind) for sha...  108 us
    ppermute x16, starting transfers between devices, flip_dp(): return lax.ppermute(value, 'dp', pairs)  20.7 us
    ppermute x12, starting transfers between devices, shift_seq(): lax.ppermute(value, 'seq', [(i, (i + step) % size) for i in range(size)])  19.4 us
    ppermute x12, starting transfers between devices, flip_step(): return lax.ppermute(value, 'dp', pairs)  13.3 us
    ppermute x16, waiting for transfers between devices, flip_dp(): return lax.ppermute(value, 'dp', pairs)  11.3 us
    pallas_call x4, Pallas kernels, pick(): pl.pallas_call(body, out_shape=[jax.ShapeDtypeStruct(shape, BF16) for sha...  10.3 us
    ppermute x2, waiting for transfers between devices, from_stretch(): lax.ppermute(jnp.where(late, first, second), BOTH, reversed_pairs(unit_pa...  8.33 us
    convert_element_type x4, other arithmetic, reduce_stages(): add_up([part[1] for part in parts]).astype(BF16)  8.28 us
  transfers between devices with their start and end apart: 54, of which 12 were waited for; matrix products, arithmetic and copies ran while one was open for 14% of the time, Pallas kernels for 31%

commit v1 on v0

--- a/solution.py
+++ b/solution.py
@@ -78,10 +78,11 @@
 
 
 def to_stretch(blocks, place):
-    odd = place["seq"] % 2 == 1
-    first = lax.ppermute(jnp.where(odd, blocks[1], blocks[0]), BOTH, unit_pairs(0))
-    second = lax.ppermute(jnp.where(odd, blocks[0], blocks[1]), BOTH, unit_pairs(1))
-    return first, second
+    return send_stretch(swapped(place["seq"] % 2 == 1, blocks))
+
+
+def send_stretch(pair):
+    return tuple(lax.ppermute(pair[n], BOTH, unit_pairs(n)) for n in range(2))
 
 
 def swapped(swap, pair):
@@ -166,20 +167,89 @@
     return own + [(tuple(m ^ 1 for m in b), tuple(m ^ 1 for m in a)) for a, b in own]
 
 
-def reduce_stages(keep, send, place, take):
+def reduce_stages(keep, send, place, segments):
     steps = len(step_bits(lax.axis_size("dp")))
-    got = yield [flip_dp(send, 1)]
-    parts = [part.reshape((2,) * steps + part.shape[1:]) for part in (keep, got[0])]
+    parts = [keep] + (yield [flip_dp(send, 1)])
     for step in range(steps):
-        got = yield [flip_step(add_up([part[1] for part in parts]).astype(BF16), step)]
-        parts = [part[0] for part in parts] + got
+        first = 1 << (steps - 1 - step)
+        parts = parts + (yield [flip_step(give_up(parts, first), step)])
+    gives = take_rows(parts, segments, place)
+    moved = yield [shift_seq(gives[j], j) for j in range(1, lax.axis_size("seq"))]
+    return add_up([gives[0]] + moved)
+
+
+def row_loop(rows, body):
+    tall = 32 if rows % 32 == 0 else rows
+
+    def step(i, carry):
+        body(pl.ds(pl.multiple_of(i * tall, tall), tall))
+        return carry
+
+    lax.fori_loop(0, rows // tall, step, 0)
+
+
+def give_kernel(*refs):
+    *parts, out_ref = refs
+
+    def some(at):
+        out_ref[0, at, :] = add_up([part[0, at, :] for part in parts]).astype(BF16)
+
+    row_loop(out_ref.shape[1], some)
+
+
+def give_up(parts, first):
+    rows, cols = parts[0].shape[1:]
+    return pl.pallas_call(
+        give_kernel,
+        grid=(first,),
+        out_shape=jax.ShapeDtypeStruct((first, rows, cols), BF16),
+        in_specs=[pl.BlockSpec((1, rows, cols), lambda n: (first + n, 0, 0))] * len(parts),
+        out_specs=pl.BlockSpec((1, rows, cols), lambda n: (n, 0, 0)),
+    )(*parts)
+
+
+def take_kernel(size, segments, seq_ref, *refs):
+    parts = refs[: len(refs) - size - 1]
+    own_ref, *out_refs = refs[len(parts) : -1]
+    total_ref = refs[-1]
+
+    def some(at):
+        total_ref[at, :] = add_up([part[0, at, :] for part in parts])
+
+    row_loop(total_ref.shape[0], some)
+    for j in range(size):
+        index = (seq_ref[0] + j) % size
+        start = 0
+        for first, rows in segments:
+            found = total_ref[pl.ds(pl.multiple_of(first + index * rows, 8), rows), :]
+            if j == 0:
+                own_ref[start : start + rows, :] = found
+            else:
+                out_refs[j - 1][start : start + rows, :] = found.astype(BF16)
+            start += rows
+
+
+def take_rows(parts, segments, place):
     size = lax.axis_size("seq")
-
-    def rows_for(j):
-        return add_up([take(part, (place["seq"] + j) % size) for part in parts])
-
-    moved = yield [shift_seq(rows_for(j).astype(BF16), j) for j in range(1, size)]
-    return add_up([rows_for(0)] + moved)
+    rows, cols = parts[0].shape[1:]
+    taken = sum(count for _, count in segments)
+    if any(first % 8 or count % 8 for first, count in segments):
+        total = add_up([part[0] for part in parts])
+        gives = []
+        for j in range(size):
+            index = (place["seq"] + j) % size
+            found = [lax.dynamic_slice_in_dim(total, f + index * count, count) for f, count in segments]
+            gives.append(jnp.concatenate(found).astype(BF16 if j else F32))
+        return gives
+    return pl.pallas_call(
+        functools.partial(take_kernel, size, segments),
+        grid=(1,),
+        out_shape=[jax.ShapeDtypeStruct((taken, cols), BF16 if j else F32) for j in range(size)],
+        in_specs=[pl.BlockSpec(memory_space=pltpu.SMEM)]
+        + [pl.BlockSpec((1, rows, cols), lambda n: (0, 0, 0))] * len(parts),
+        out_specs=[pl.BlockSpec((taken, cols), lambda n: (0, 0))] * size,
+        scratch_shapes=[pltpu.VMEM((rows, cols), F32)],
+    )(place["seq"][None], *parts)
 
 
 def add_up(parts):
@@ -336,7 +406,7 @@
     one, two = to_stretch(blocks, place)
     one = (yield [one])[0]
     two = (yield [two])[0]
-    return jnp.concatenate(swapped(place["micro"] == 1, (one, two)))
+    return one, two
 
 
 def output_stages(out, routes, place):
@@ -434,14 +504,26 @@
     return w_ref[:, CHANNELS:].astype(F32).T[HEADS : HEADS + 1]
 
 
-def project_kernel(plan, rows, scal, x_ref, cw_ref, cb_ref, dl_ref, sb_ref, *refs):
+def join_blocks(late, one_ref, two_ref, out_ref, start):
+    rows = one_ref.shape[0]
+    for turn, pair in enumerate(((one_ref, two_ref), (two_ref, one_ref))):
+
+        @pl.when(late == turn)
+        def _():
+            for n, block_ref in enumerate(pair):
+                out_ref[start + n * rows : start + (n + 1) * rows, :] = block_ref[...]
+
+
+def project_kernel(plan, rows, scal, one_ref, two_ref, halo_ref, cw_ref, cb_ref, dl_ref, sb_ref, *refs):
     count = PIECES
     pieces = refs[:count]
-    nh_ref, cext_ref, act_ref, step_ref, sig_ref, cum_ref = refs[count : count + 6]
-    w_ref, proj_ref, sem = refs[count + 6 :]
+    x_ref, nh_ref, cext_ref, act_ref, step_ref, sig_ref, cum_ref = refs[count : count + 7]
+    w_ref, proj_ref, sem = refs[count + 7 :]
     copies = start_pieces(scal[0], pieces, plan, w_ref, sem, rows)
     total = x_ref.shape[0]
     length = total - HALO
+    x_ref[0:HALO, :] = halo_ref[...]
+    join_blocks(scal[2], one_ref, two_ref, x_ref, HALO)
     chunks = length // CHUNK
 
     tall = 3 * HALO if total % (3 * HALO) == 0 else HALO
@@ -548,20 +630,48 @@
     lax.fori_loop(0, chunks, chunk, 0)
 
 
-def middle_kernel(gate_plan, plan, rows, scal, local_ref, act_ref, step_ref, cum_ref, nh_ref, state_ref, x_ref,
-                  c_ref, skip_ref, *refs):
+def core_kernel(local_ref, act_ref, step_ref, cum_ref, state_ref, core_ref, states_ref, state_s, wide_ref, expand_ref):
+    chunks = act_ref.shape[0] // CHUNK
+    fill_expander(expand_ref)
+    state_s[...] = state_ref[...].astype(F32)
+
+    def chunk(c, carry):
+        at = pl.ds(pl.multiple_of(c * CHUNK, CHUNK), CHUNK)
+        in_keys = act_ref[at, INNER : INNER + STATE]
+        out_keys = act_ref[at, INNER + STATE : CHANNELS]
+        cum = cum_ref[at, :]
+        last = cum[CHUNK - 1 : CHUNK]
+        weight = jnp.exp(last - cum) * step_ref[at, :]
+        small = jnp.concatenate([jnp.exp(cum), weight, jnp.broadcast_to(jnp.exp(last), (8, LANES))], axis=0)
+        wide_ref[...] = dot(jnp.concatenate(two_parts(small), axis=1), expand_ref[...])
+        state_b = state_s[...].astype(BF16)
+        states_ref[c] = state_b
+        for tile in range(INNER // LANES):
+            cols = slice(tile * LANES, (tile + 1) * LANES)
+            values = act_ref[at, cols].astype(F32)
+            core_ref[at, cols] = local_ref[at, cols] + wide_ref[0:CHUNK, cols] * dot(out_keys, state_b[:, cols])
+            weighted = (wide_ref[CHUNK : 2 * CHUNK, cols] * values).astype(BF16)
+            state_s[:, cols] = wide_ref[2 * CHUNK : 2 * CHUNK + 1, cols] * state_s[:, cols] + dot(
+                in_keys, weighted, 0, 0
+            )
+        return carry
+
+    lax.fori_loop(0, chunks, chunk, 0)
+
+
+def middle_kernel(gate_plan, plan, rows, scal, core_ref, act_ref, cum_ref, nh_ref, x_ref, one_ref, two_ref, skip_ref,
+                  *refs):
     count = PIECES
-    out_ref, gn_ref, dgate_ref, gcore_ref, rowq_ref, lsg_ref, states_ref, gskip_ref = refs[
-        count : count + 8
-    ]
-    (w_ref, wg_ref, gate_ref, gain_ref, mc_ref, gno_ref, state_s, wide_ref, core_ref, mixed_ref, acc_ref, expand_ref,
-     gate_sem, sem) = refs[count + 8 :]
+    c_ref, out_ref, gn_ref, dgate_ref, gcore_ref, rowq_ref, lsg_ref, gskip_ref = refs[count : count + 8]
+    (w_ref, wg_ref, gate_ref, gain_ref, mc_ref, gno_ref, wide_ref, mixed_ref, sig_ref, gated_ref, acc_ref, expand_ref, gate_sem,
+     sem) = refs[count + 8 :]
     gate_copies = start_pieces(scal[0], refs[:count], gate_plan, wg_ref, gate_sem, rows)
     copies = start_pieces(scal[0], refs[:count], plan, w_ref, sem, rows)
     length = act_ref.shape[0]
     chunks = length // CHUNK
     tiles = INNER // LANES
     model = c_ref.shape[1]
+    join_blocks(scal[2], one_ref, two_ref, c_ref, 0)
     fill_expander(expand_ref)
 
     def mask(i, carry):
@@ -589,46 +699,30 @@
 
     lax.fori_loop(0, INNER // 384, back_project, 0)
     gain_ref[...] = w_ref[:, model:].astype(F32).T[0:8]
-    state_s[...] = state_ref[...].astype(F32)
     acc_ref[...] = jnp.zeros_like(acc_ref)
     gskip_ref[...] = jnp.zeros_like(gskip_ref)
 
     def chunk(c, before):
         at = pl.ds(pl.multiple_of(c * CHUNK, CHUNK), CHUNK)
-        in_keys = act_ref[at, INNER : INNER + STATE]
         out_keys = act_ref[at, INNER + STATE : CHANNELS]
         cum = cum_ref[at, :]
-        last = cum[CHUNK - 1 : CHUNK]
-        growth = jnp.exp(cum)
-        weight = jnp.exp(last - cum) * step_ref[at, :]
-        small = jnp.concatenate(
-            [growth, weight, jnp.exp(cum + before), jnp.broadcast_to(jnp.exp(last), (8, LANES))], axis=0
-        )
-        wide_ref[...] = dot(jnp.concatenate(two_parts(small), axis=1), expand_ref[...])
-        state_b = state_s[...].astype(BF16)
-        states_ref[c] = state_b
+        wide_ref[...] = dot(jnp.concatenate(two_parts(jnp.exp(cum + before)), axis=1), expand_ref[...])
         squares = jnp.zeros((CHUNK, LANES), F32)
         for tile in range(tiles):
             cols = slice(tile * LANES, (tile + 1) * LANES)
-            values = act_ref[at, cols].astype(F32)
-            readout = dot(out_keys, state_b[:, cols])
-            core = local_ref[at, cols] + wide_ref[0:CHUNK, cols] * readout
-            mixed = core + skip_ref[0:1, cols] * values
-            core_ref[:, cols] = core
+            mixed = core_ref[at, cols] + skip_ref[0:1, cols] * act_ref[at, cols].astype(F32)
             mixed_ref[:, cols] = mixed
             gate = gate_ref[at, cols]
-            gated = mixed * (gate * jax.nn.sigmoid(gate))
+            sig = jax.nn.sigmoid(gate)
+            gated = mixed * (gate * sig)
+            sig_ref[:, cols] = sig
+            gated_ref[:, cols] = gated
             squares = squares + gated * gated
-            weighted = (wide_ref[CHUNK : 2 * CHUNK, cols] * values).astype(BF16)
-            state_s[:, cols] = wide_ref[3 * CHUNK : 3 * CHUNK + 1, cols] * state_s[:, cols] + dot(
-                in_keys, weighted, 0, 0
-            )
         scale = lax.rsqrt(jnp.sum(squares, axis=1, keepdims=True) / INNER + EPSILON)
         products = jnp.zeros((CHUNK, LANES), F32)
         for tile in range(tiles):
             cols = slice(tile * LANES, (tile + 1) * LANES)
-            gate = gate_ref[at, cols]
-            gn = mixed_ref[:, cols] * (gate * jax.nn.sigmoid(gate)) * scale
+            gn = gated_ref[:, cols] * scale
             gain = gain_ref[0:1, cols]
             gn_ref[at, cols] = (gn * gain).astype(BF16)
             products = products + gn * (gno_ref[at, cols] * gain)
@@ -637,10 +731,10 @@
         for tile in range(tiles):
             cols = slice(tile * LANES, (tile + 1) * LANES)
             gate = gate_ref[at, cols]
-            sig = jax.nn.sigmoid(gate)
+            sig = sig_ref[:, cols]
             silu = gate * sig
             mixed = mixed_ref[:, cols]
-            dgated = scale * (gno_ref[at, cols] * gain_ref[0:1, cols] - (mixed * silu * scale) * mean)
+            dgated = scale * (gno_ref[at, cols] * gain_ref[0:1, cols] - (gated_ref[:, cols] * scale) * mean)
             g = dgated * silu
             dgate_ref[at, cols] = (dgated * mixed * (sig * (1.0 + gate * (1.0 - sig)))).astype(BF16)
             gcore = g.astype(BF16)
@@ -650,11 +744,11 @@
                 (g * values).reshape(CHUNK // 8, 8, LANES), axis=0
             )
             gcore_f = gcore.astype(F32)
-            rowq = rowq + head_sums(gcore_f * core_ref[:, cols], tile)
-            scaled = (wide_ref[2 * CHUNK : 3 * CHUNK, cols] * gcore_f).astype(BF16)
+            rowq = rowq + head_sums(gcore_f * core_ref[at, cols], tile)
+            scaled = (wide_ref[:, cols] * gcore_f).astype(BF16)
             acc_ref[:, cols] = acc_ref[:, cols] + dot(out_keys, scaled, 0, 0)
         rowq_ref[at, :] = rowq
-        return before + last
+        return before + cum[CHUNK - 1 : CHUNK]
 
     lax.fori_loop(0, chunks, chunk, jnp.zeros((1, LANES), F32))
     lsg_ref[...] = acc_ref[...].astype(BF16)
@@ -978,23 +1072,23 @@
     taps = jnp.pad(conv_weight, ((0, 8 - KCONV), (0, 0)))
     skip_row = jnp.repeat(skip_gain, HDIM)[None]
     n_valid = jnp.clip(own_length - place["turn"] * length, 0, length)
-    scal = jnp.stack([dp, n_valid])
+    scal = jnp.stack([dp, n_valid, place["micro"]])
     rows_of = (taps, conv_bias[None], lane_row(decay_log), lane_row(step_bias), skip_row, scal)
 
     shards = Chain(seq_stages(conv_shard, place))
-    tok = advance(tok, shards, *moving)
+    tok = advance(swapped(place["seq"] % 2 == 1, tok), shards, *moving)
     conv_z = shards.value
     conv = Chain(spread_stages(conv_z.reshape(rows, WIDTH)))
-    one, two = to_stretch(tok, place)
+    one, two = send_stretch(tok)
     one, two, rows_of, rest_shard = advance((one, two, rows_of, rest_shard), conv, *moving)
     taps, conv_bias_row, decay_row, bias_row, skip_row, scal = rows_of
-    first, second = swapped(place["micro"] == 1, (one, two))
-    halo = lax.ppermute(second[block_len - HALO :], BOTH, neighbour_pairs(1))
-    first, second, halo = advance((first, second, halo), conv, *moving)
+    late = place["micro"] == 1
+    tail = jnp.where(late, one[block_len - HALO :], two[block_len - HALO :])
+    halo = lax.ppermute(tail, BOTH, neighbour_pairs(1))
+    one, two, halo = advance((one, two, halo), conv, *moving)
     shards = Chain(seq_stages(rest_shard, place))
     while conv.pending is not None:
         halo = advance(halo, conv, *moving)
-    x_ext = jnp.concatenate([halo, first, second])
     conv_pieces = conv.value
     gain_rows = jnp.swapaxes(conv_z[:, :, CHANNELS + HEADS + 1 : CHANNELS + HEADS + 3], 1, 2)
     gain_rows = jnp.pad(gain_rows.reshape(2 * rows, 1), ((0, 0), (0, LANES - 1)))
@@ -1006,13 +1100,13 @@
     made = call(
         functools.partial(project_kernel, conv_plan, rows),
         scal,
-        [x_ext, taps, conv_bias_row, decay_row, bias_row],
+        [one, two, halo, taps, conv_bias_row, decay_row, bias_row],
         conv_pieces,
-        [((length + HALO, model), BF16), ((length + HALO, CHANNELS), BF16), ((length, CHANNELS), BF16)]
+        [((length + HALO, model), BF16)] * 2 + [((length + HALO, CHANNELS), BF16), ((length, CHANNELS), BF16)]
         + [((length, LANES), F32)] * 3,
         [pltpu.VMEM((model, WIDTH), BF16), pltpu.VMEM((length + HALO, WIDTH), F32), sems(conv_plan)],
     )
-    nh, cext, act, step, sig, cum = advance(made, *moving)
+    x_ext, nh, cext, act, step, sig, cum = advance(made, *moving)
     rest_z = shards.value
     gate_z = [rest_z[:, :, n * model : (n + 1) * model].reshape(rows, model) for n in range(2)]
     out_z = jnp.concatenate([rest_z[:, :, INNER : INNER + model], rest_z[:, :, INNER + model :]], axis=1)
@@ -1040,27 +1134,39 @@
         return jnp.zeros_like(own) if carried is None else carried
 
     state_in = relay(update, neighbour_pairs(1))
+    core, states = advance(
+        call(
+            core_kernel,
+            None,
+            [local, act, step, cum, state_in],
+            [],
+            [(wide, F32), ((length // CHUNK, STATE, INNER), BF16)],
+            [pltpu.VMEM((STATE, INNER), F32), pltpu.VMEM((2 * CHUNK + 8, INNER), F32),
+             pltpu.VMEM((2 * LANES, INNER), BF16)],
+        ),
+        *moving,
+    )
     while rest.pending is not None:
-        state_in = advance(state_in, *moving)
+        advance((), *moving)
     if dealt:
         while cot_chain.pending is not None:
             advance((), cot_chain)
-        c_own = cot_chain.value
+        c_pair = cot_chain.value
     else:
-        c_own = jnp.concatenate(swapped(place["micro"] == 1, to_stretch(cot_given, place)))
+        c_pair = to_stretch(cot_given, place)
     rest_pieces = rest.value
 
-    out, gn, dgate, gcore, rowq, lsg, states, gskip = call(
+    c_own, out, gn, dgate, gcore, rowq, lsg, gskip = call(
         functools.partial(middle_kernel, gate_plan, out_plan, rows),
         scal,
-        [local, act, step, cum, nh, state_in, x_ext, c_own, skip_row],
+        [core, act, cum, nh, x_ext, *c_pair, skip_row],
         rest_pieces,
-        [((length, model), BF16), (wide, BF16), (wide, BF16), (wide, BF16), ((length, LANES), F32),
-         ((STATE, INNER), BF16), ((length // CHUNK, STATE, INNER), BF16), ((8, INNER), F32)],
+        [((length, model), BF16)] * 2 + [(wide, BF16), (wide, BF16), (wide, BF16), ((length, LANES), F32),
+         ((STATE, INNER), BF16), ((8, INNER), F32)],
         [pltpu.VMEM((INNER, model + LANES), BF16), pltpu.VMEM((model, INNER), BF16), pltpu.VMEM(wide, F32),
          pltpu.VMEM((8, INNER), F32), pltpu.VMEM((length, model), BF16), pltpu.VMEM(wide, F32),
-         pltpu.VMEM((STATE, INNER), F32), pltpu.VMEM((3 * CHUNK + 8, INNER), F32),
-         pltpu.VMEM((CHUNK, INNER), F32), pltpu.VMEM((CHUNK, INNER), F32), pltpu.VMEM((STATE, INNER), F32),
+         pltpu.VMEM((CHUNK, INNER), F32), pltpu.VMEM((CHUNK, INNER), F32), pltpu.VMEM((CHUNK, INNER), F32),
+         pltpu.VMEM((CHUNK, INNER), F32), pltpu.VMEM((STATE, INNER), F32),
          pltpu.VMEM((2 * LANES, INNER), BF16), sems(gate_plan), sems(out_plan)],
     )
     if dealt:
@@ -1086,13 +1192,8 @@
         *moving,
     )
 
-    def early_take(part, index):
-        gates = part[: 2 * rows].reshape(2, size, shard_rows, model)
-        gates = lax.dynamic_index_in_dim(gates, index, 1, keepdims=False).reshape(2 * shard_rows, model)
-        outs = part[2 * rows :].reshape(size, 2 * shard_rows, model)
-        return jnp.concatenate([gates, lax.dynamic_index_in_dim(outs, index, 0, keepdims=False)])
-
-    early = Chain(reduce_stages(keep1, send1, place, early_take))
+    early_segments = [(0, shard_rows), (rows, shard_rows), (2 * rows, 2 * shard_rows)]
+    early = Chain(reduce_stages(keep1, send1, place, early_segments))
     moving.append(early)
     made = call(
         functools.partial(local_back_kernel, gate_plan, rows),
@@ -1131,10 +1232,7 @@
         *moving,
     )
 
-    def late_take(part, index):
-        return lax.dynamic_index_in_dim(part.reshape(size, shard_rows, WIDTH), index, 0, keepdims=False)
-
-    final = Chain(reduce_stages(keep2, send2, place, late_take))
+    final = Chain(reduce_stages(keep2, send2, place, [(0, shard_rows)]))
     moving.append(final)
     (gtok,) = advance(
         call(
@@ -1149,8 +1247,8 @@
     )
 
     one, two = from_stretch(gtok[:block_len], gtok[block_len:], place)
-    one = advance(one, *moving)
-    back = one, advance(two, *moving)
+    one = advance(one, sums, final)
+    back = one, advance(two, sums, final)
     while any(chain.pending is not None for chain in moving):
         advance((), *moving)
     grad_tokens = jnp.stack(swapped(place["seq"] % 2 == 1, back))

time: 296 us -> 287 us (0.970)
  Pallas kernels: 120 us -> 138 us
  other arithmetic: 31.2 us -> 17.6 us
  local copies, waits for them, and re-layouts: 29.2 us -> 20.4 us
  starting transfers between devices: 76.2 us -> 72.9 us
    pallas_call x0 -> x6, Pallas kernels: none -> 14.6 us  [the longest x4 9.42 us: give_up(): pl.pallas_call(give_kernel, grid=(first,), out_shape=jax.ShapeDtypeStruct...]
    convert_element_type x7 -> x0, other arithmetic: 9.84 us -> none  [the longest x4 8.28 us: reduce_stages(): add_up([part[1] for part in parts]).astype(BF16)]
    ppermute x16, starting transfers between devices: 20.7 us -> 12.8 us  [flip_dp(): return lax.ppermute(value, 'dp', pairs)]
    slice x8 -> x0, local copies, waits for them, and re-layouts: 6.97 us -> none  [the longest x4 4.83 us: early_take(): gates = part[:2 * rows].reshape(2, size, shard_rows, model)]
    ppermute x12, waiting for transfers between devices: 2.22 us -> 7.74 us  [flip_step(): return lax.ppermute(value, 'dp', pairs)]
    unnamed x104 -> x102, local copies, waits for them, and re-layouts: 5.08 us -> 9.78 us
    pallas_call x8 -> x9, Pallas kernels: 108 us -> 112 us  [call(): pl.pallas_call(body, out_shape=[jax.ShapeDtypeStruct(shape, kind) for sha...]
    ppermute x2, starting transfers between devices: 3.7 us -> 6.71 us  [from_stretch(): lax.ppermute(jnp.where(late, first, second), BOTH, reversed_pairs(unit_pa...]
  transfers between devices with their start and end apart: 54 -> 54, of which waited for: 12 -> 13; matrix products, arithmetic and copies ran while one was open for 14% -> 7% of each run, Pallas kernels for 31% -> 39%
where the time goes in v1:
time: 287 us; the launch traced here: 286 us
  Pallas kernels  138 us (48%)
  starting transfers between devices  72.9 us (25%)
  waiting for transfers between devices  34.8 us (12%)
  local copies, waits for them, and re-layouts  20.4 us (7%)
  other arithmetic  17.6 us (6%)
    pallas_call x9, Pallas kernels, call(): pl.pallas_call(body, out_shape=[jax.ShapeDtypeStruct(shape, kind) for sha...  112 us
    ppermute x12, starting transfers between devices, shift_seq(): lax.ppermute(value, 'seq', [(i, (i + step) % size) for i in range(size)])  21.3 us
    ppermute x12, starting transfers between devices, flip_step(): return lax.ppermute(value, 'dp', pairs)  15 us
    ppermute x16, starting transfers between devices, flip_dp(): return lax.ppermute(value, 'dp', pairs)  12.8 us
    ppermute x16, waiting for transfers between devices, flip_dp(): return lax.ppermute(value, 'dp', pairs)  12.5 us
    pallas_call x4, Pallas kernels, pick(): pl.pallas_call(body, out_shape=[jax.ShapeDtypeStruct(shape, BF16) for sha...  10.2 us
    unnamed x102, local copies, waits for them, and re-layouts  9.78 us
    pallas_call x4, Pallas kernels, give_up(): pl.pallas_call(give_kernel, grid=(first,), out_shape=jax.ShapeDtypeStruct...  9.42 us
  transfers between devices with their start and end apart: 54, of which 13 were waited for; matrix products, arithmetic and copies ran while one was open for 7% of the time, Pallas kernels for 39%

profile of v1, /device:TPU:0, one launch (start us, length us, event | category | flops | bytes accessed | tf_op | source)
XLA Modules:
  0.0 285.8 jit_solution(2217323276676432239)
XLA Ops:
  3.4 5.1 %collective-permute-start.5 = (bf16[24,1920]{1,0:T(8,128)(2,1)S(1)}, bf16[24,1920]{1,0:T(8,128)(2,1)S(1)}, u32[]{:S(2)}, u32[]{:S(2)}) collective-permute-start(bf16[24,1920]{1,0:T(8,128)(2,1)S(1)} %pad.19), channel_id=1, source_target_pairs={{0,3},{1,0},{2,1},{3,2},{4,7},{5,4},{6,5},{7,6},{8,11},{9,8},{10,9... | collective-permute-start | bytes 276488 | tf_op jit(solution)/shard_map/ppermute | solution.py:46
  24.8 8.0 %collective-permute-done.1 = s32[2,4]{1,0:T(2,128)S(1)} collective-permute-done((s32[2,4]{1,0:T(2,128)S(1)}, s32[2,4]{1,0:T(2,128)S(1)}, u32[]{:S(2)}, u32[]{:S(2)}) %collective-permute-start.1) | collective-permute-done | bytes 64 | tf_op jit(solution)/shard_map/ppermute | solution.py:30
  52.2 2.8 collective-permute-done.12.refs_1_
  62.0 13.4 %shard_map.214 = (bf16[528,768]{1,0:T(8,128)(2,1)}, bf16[528,768]{1,0:T(8,128)(2,1)}, bf16[528,1792]{1,0:T(8,128)(2,1)}, bf16[512,1792]{1,0:T(8,128)(2,1)}, f32[...) custom-call(s32[3]{0:T(128)} %pad_add_fusion.4.scal, bf16[256,768]{1,0:T(8,128)(2,1)} %copy-done.23, ...), custom_call_target="tpu_custom_call" | custom-call | tf_op jit(solution)/shard_map/pallas_call | solution.py:1015
  76.3 2.7 shard_map.216
  83.6 7.6 %shard_map.215 = (f32[512,1536]{1,0:T(8,128)}, bf16[128,1536]{1,0:T(8,128)(2,1)}, f32[8,128]{1,0:T(8,128)}) custom-call(bf16[512,1792]{1,0:T(8,128)(2,1)} %get-tuple-element.170.act_ref, f32[512,128]{1,0:T(8,128)} %get-tuple-element.171.step_ref, f32[512,128]{1,0:T(8,128)} %get-tuple-element.172.cum_ref), custom_call_target="tpu_custom_call" | custom-call | tf_op jit(solution)/shard_map/pallas_call | solution.py:1015
  92.0 5.4 %collective-permute-start.25 = (bf16[2,192,1664]{2,1,0:T(8,128)(2,1)S(1)}, bf16[2,192,1664]{2,1,0:T(8,128)(2,1)S(1)}, u32[]{:S(2)}, u32[]{:S(2)}) collective-permute-start(bf16[2,192,1664]{2,1,0:T(8,128)(2,1)S(1)} %pad_maximum_fusion.refs_0_), channel_id=1, source_target_pairs={{0,4},{4,0},{8,12},{12,8},{16,20},{20,16},{24,28},{28,24},{1,5},{5... | collective-permute-start | bytes 3833864 | tf_op jit(solution)/shard_map/ppermute | solution.py:30
  98.4 2.9 %collective-permute-start.22 = (bf16[128,1536]{1,0:T(8,128)(2,1)S(1)}, bf16[128,1536]{1,0:T(8,128)(2,1)}, u32[]{:S(2)}, u32[]{:S(2)}) collective-permute-start(bf16[128,1536]{1,0:T(8,128)(2,1)S(1)} %copy-done.49), channel_id=1, source_target_pairs={{0,4},{1,5},{2,6},{3,7},{8,12},{9,13},{10,14},{11,15},{16,20},{17,... | collective-permute-start | bytes 1179656 | tf_op jit(solution)/shard_map/ppermute | solution.py:1133
  102.0 7.4 %shard_map.217 = (f32[512,1536]{1,0:T(8,128)}, bf16[4,128,1536]{2,1,0:T(8,128)(2,1)}) custom-call(f32[512,1536]{1,0:T(8,128)} %get-tuple-element.181.local_ref, bf16[512,1792]{1,0:T(8,128)(2,1)} %get-tuple-element.170.act_ref, f32[512,128]{1,0:T(8,128)} %get-tuple-element.171.step_ref, f32[512,128]{1,0:T(8,128)} %get-tuple-element.172.cum_ref, ...), custom_call_target="tpu_custom_call" | custom-call | tf_op jit(solution)/shard_map/pallas_call | solution.py:1015
  109.4 4.2 %collective-permute-done.23.two_ref = bf16[256,768]{1,0:T(8,128)(2,1)} collective-permute-done((bf16[256,768]{1,0:T(8,128)(2,1)}, bf16[256,768]{1,0:T(8,128)(2,1)}, u32[]{:S(2)}, u32[]{:S(2)}) %collective-permute-start.23) | collective-permute-done | bytes 393248 | tf_op jit(solution)/shard_map/ppermute | solution.py:85
  114.7 3.0 %collective-permute-done.26.refs_3_ = bf16[2,192,1664]{2,1,0:T(8,128)(2,1)S(1)} collective-permute-done((bf16[2,192,1664]{2,1,0:T(8,128)(2,1)S(1)}, bf16[2,192,1664]{2,1,0:T(8,128)(2,1)S(1)}, u32[]{:S(2)}, u32[]{:S(2)}) %collective-permute-start.26) | collective-permute-done | bytes 1277984 | tf_op jit(solution)/shard_map/ppermute | solution.py:30
  118.7 21.8 %shard_map.218 = (bf16[512,768]{1,0:T(8,128)(2,1)}, bf16[512,768]{1,0:T(8,128)(2,1)}, bf16[512,1536]{1,0:T(8,128)(2,1)}, bf16[512,1536]{1,0:T(8,128)(2,1)}, bf16...) custom-call(s32[3]{0:T(128)} %pad_add_fusion.4.scal, ...), custom_call_target="tpu_custom_call" | custom-call | tf_op jit(solution)/shard_map/pallas_call | solution.py:1015
  142.4 10.7 %shard_map.219 = (bf16[4,384,768]{2,1,0:T(8,128)(2,1)}, bf16[4,384,768]{2,1,0:T(8,128)(2,1)}) custom-call(s32[3]{0:T(128)} %pad_add_fusion.4.scal, bf16[512,1536]{1,0:T(8,128)(2,1)} %get-tuple-element.194.gn_ref, bf16[512,768]{1,0:T(8,128)(2,1)} %get-tuple-element.195.c_ref, bf16[528,768]{1,0:T(8,128)(2,1)} %get-tuple-element.187.nh_ref, ...), custom_call_target="tpu_custom_call" | custom-call | tf_op jit(solution)/shard_map/pallas_call | solution.py:1015
  157.7 12.3 %shard_map.220 = (f32[512,1536]{1,0:T(8,128)}, f32[512,256]{1,0:T(8,128)}, f32[512,768]{1,0:T(8,128)}) custom-call(s32[3]{0:T(128)} %pad_add_fusion.4.scal, bf16[512,1792]{1,0:T(8,128)(2,1)} %get-tuple-element.170.act_ref, f32[512,128]{1,0:T(8,128)} %get-tuple-element.171.step_ref, f32[512,128]{1,0:T(8,128)} %get-tuple-element.172.cum_ref, ...), custom_call_target="tpu_custom_call" | custom-call | tf_op jit(solution)/shard_map/pallas_call | solution.py:1015
  171.6 2.6 shard_map.222
  176.0 19.0 %shard_map.221 = (f32[512,1792]{1,0:T(8,128)}, f32[16,1792]{1,0:T(8,128)}, bf16[512,128]{1,0:T(8,128)(2,1)}, f32[8,1920]{1,0:T(8,128)}) custom-call(bf16[512,1792]{1,0:T(8,128)(2,1)} %get-tuple-element.170.act_ref, f32[512,128]{1,0:T(8,128)} %get-tuple-element.171.step_ref, f32[512,128]{1,0:T(8,128)} %get-tuple-element.210.sig_ref, ...), custom_call_target="tpu_custom_call" | custom-call | tf_op jit(solution)/shard_map/pallas_call | solution.py:1015
  204.2 10.2 %shard_map.223 = (bf16[512,1920]{1,0:T(8,128)(2,1)}, bf16[4,96,1920]{2,1,0:T(8,128)(2,1)}, bf16[4,96,1920]{2,1,0:T(8,128)(2,1)}) custom-call(s32[3]{0:T(128)} %pad_add_fusion.4.scal, f32[512,1792]{1,0:T(8,128)} %get-tuple-element.225.gconv_ref, f32[16,1792]{1,0:T(8,128)} %copy-done.40, bf16[512,128]{1,0:T(8,128)(2,1)} %get-tuple-element.227.graw_ref, ...), custom_call_target="tpu_custom_call" | custom-call | tf_op jit(solution)/shard_map/pallas_call | solution.py:1015
  220.7 2.9 %shard_map.227 = (f32[96,768]{1,0:T(8,128)}, bf16[96,768]{1,0:T(8,128)(2,1)}, bf16[96,768]{1,0:T(8,128)(2,1)}, bf16[96,768]{1,0:T(8,128)(2,1)}) custom-call(s32[1]{0:T(128)} %bitcast.39.seq_ref, bf16[4,384,768]{2,1,0:T(8,128)(2,1)} %get-tuple-element.222.refs_0_, bf16[4,384,768]{2,1,0:T(8,128)(2,1)} %copy-done, bf16[2,384,768]{2,1,0:T(8,128)(2,1)} %copy-done.8, ...), custom_call_target="tpu_custom_call" | custom-call | tf_op jit(solution)/shard_map/pallas_call | solution.py:244
  227.7 9.2 %shard_map.225 = bf16[512,768]{1,0:T(8,128)(2,1)} custom-call(s32[3]{0:T(128)} %pad_add_fusion.4.scal, bf16[512,1920]{1,0:T(8,128)(2,1)} %get-tuple-element.234.gproj_ref, f32[512,768]{1,0:T(8,128)} %get-tuple-element.235.gng_ref, bf16[528,768]{1,0:T(8,128)(2,1)} %get-tuple-element.188.x_ref, bf16[512,768]{1,0:T(8,128)(2,1)} %get-tuple-element.195.c_ref, ...), custom_call_target="tpu_custom_call" | custom-call | tf_op jit(solution)/shard_map/pallas_call | solution.py:1015
  244.5 4.9 %collective-permute-start.48 = (bf16[256,768]{1,0:T(8,128)(2,1)S(1)}, bf16[256,768]{1,0:T(8,128)(2,1)S(1)}, u32[]{:S(2)}, u32[]{:S(2)}) collective-permute-start(bf16[256,768]{1,0:T(8,128)(2,1)S(1)} %get-tuple-element.297), channel_id=1, source_target_pairs={{2,0},{0,1},{6,2},{4,3},{3,4},{1,5},{7,6},{5,7},{10,8},{8,9},{14,1... | collective-permute-start | bytes 1179656 | tf_op jit(solution)/shard_map/ppermute | solution.py:95
  249.4 3.8 %collective-permute-done.47.refs_2_ = bf16[2,96,1920]{2,1,0:T(8,128)(2,1)S(1)} collective-permute-done((bf16[2,96,1920]{2,1,0:T(8,128)(2,1)}, bf16[2,96,1920]{2,1,0:T(8,128)(2,1)S(1)}, u32[]{:S(2)}, u32[]{:S(2)}) %collective-permute-start.47) | collective-permute-done | bytes 737312 | tf_op jit(solution)/shard_map/ppermute | solution.py:41
  259.6 2.7 shard_map.228
  262.4 5.5 %collective-permute-done.48 = bf16[256,768]{1,0:T(8,128)(2,1)S(1)} collective-permute-done((bf16[256,768]{1,0:T(8,128)(2,1)S(1)}, bf16[256,768]{1,0:T(8,128)(2,1)S(1)}, u32[]{:S(2)}, u32[]{:S(2)}) %collective-permute-start.48) | collective-permute-done | bytes 393248 | tf_op jit(solution)/shard_map/ppermute | solution.py:95
  271.8 4.4 %collective-permute-start.51 = (bf16[24,1920]{1,0:T(8,128)(2,1)}, bf16[24,1920]{1,0:T(8,128)(2,1)S(1)}, u32[]{:S(2)}, u32[]{:S(2)}) collective-permute-start(bf16[24,1920]{1,0:T(8,128)(2,1)} %get-tuple-element.251), channel_id=1, source_target_pairs={{0,1},{1,2},{2,3},{3,0},{4,5},{5,6},{6,7},{7,4},{8,9},{9,10},{10,1... | collective-permute-start | bytes 276488 | tf_op jit(solution)/shard_map/ppermute | solution.py:46
  (276 shorter events, 110.9 us)
Async XLA Ops:
  10.2 13.0 %collective-permute-start = (s32[1,4]{1,0:T(1,128)S(1)}, s32[1,4]{1,0:T(1,128)S(1)}, u32[]{:S(2)}, u32[]{:S(2)}) collective-permute-start(s32[1,4]{1,0:T(1,128)S(1)} %add_bitcast_fusion), channel_id=1, source_target_pairs={{0,4},{4,0},{8,12},{12,8},{16,20},{20,16},{24,28},{28,24},{1,5},{5... | collective-permute-start | bytes 56 | tf_op jit(solution)/shard_map/ppermute | solution.py:30
  16.8 24.5 %collective-permute-start.10 = (bf16[2,2,128,768]{3,2,0,1:T(8,128)(2,1)S(1)}, bf16[2,2,128,768]{3,2,0,1:T(8,128)(2,1)S(1)}, u32[]{:S(2)}, u32[]{:S(2)}) collective-permute-start(bf16[2,2,128,768]{3,2,0,1:T(8,128)(2,1)S(1)} %pad_maximum_fusion.1), channel_id=1, source_target_pairs={{0,8},{4,20},{8,0},{12,28},{16,24},{20,4},{24,16},{28,12},{1,9},{5... | collective-permute-start | bytes 2359304 | tf_op jit(solution)/shard_map/ppermute | solution.py:41
  18.5 22.7 %collective-permute-start.9 = (bf16[1,96,1920]{2,1,0:T(8,128)(2,1)S(1)}, bf16[1,96,1920]{2,1,0:T(8,128)(2,1)}, u32[]{:S(2)}, u32[]{:S(2)}) collective-permute-start(bf16[1,96,1920]{2,1,0:T(8,128)(2,1)S(1)} %bitcast.78), channel_id=1, source_target_pairs={{0,8},{4,20},{8,0},{12,28},{16,24},{20,4},{24,16},{28,12},{1,9},{5... | collective-permute-start | bytes 1105928 | tf_op jit(solution)/shard_map/ppermute | solution.py:41
  19.1 22.1 %collective-permute-start.7 = (bf16[256,768]{1,0:T(8,128)(2,1)}, bf16[256,768]{1,0:T(8,128)(2,1)S(1)}, u32[]{:S(2)}, u32[]{:S(2)}) collective-permute-start(bf16[256,768]{1,0:T(8,128)(2,1)} %get-tuple-element.139), channel_id=1, source_target_pairs={{0,0},{1,2},{2,4},{3,6},{4,1},{5,3},{6,5},{7,7},{8,8},{9,10},{10,1... | collective-permute-start | bytes 1179656 | tf_op jit(solution)/shard_map/ppermute | solution.py:85
  20.7 20.5 %collective-permute-start.8 = (bf16[256,768]{1,0:T(8,128)(2,1)S(1)}, bf16[256,768]{1,0:T(8,128)(2,1)S(1)}, u32[]{:S(2)}, u32[]{:S(2)}) collective-permute-start(bf16[256,768]{1,0:T(8,128)(2,1)S(1)} %get-tuple-element.140), channel_id=1, source_target_pairs={{0,2},{1,0},{2,6},{3,4},{4,3},{5,1},{6,7},{7,5},{8,10},{9,8},{10,1... | collective-permute-start | bytes 1179656 | tf_op jit(solution)/shard_map/ppermute | solution.py:85
  55.0 20.4 %collective-permute-start.15 = (bf16[2,2,128,768]{3,2,1,0:T(8,128)(2,1)}, bf16[2,2,128,768]{3,2,1,0:T(8,128)(2,1)S(1)}, u32[]{:S(2)}, u32[]{:S(2)}) collective-permute-start(bf16[2,2,128,768]{3,2,1,0:T(8,128)(2,1)} %shard_map.213), channel_id=1, source_target_pairs={{0,16},{4,12},{8,24},{12,4},{16,0},{20,28},{24,8},{28,20},{1,17},{... | collective-permute-start | bytes 2359304 | tf_op jit(solution)/shard_map/ppermute | solution.py:41
  56.6 18.8 %collective-permute-start.18 = (bf16[24,3072]{1,0:T(8,128)(2,1)}, bf16[24,3072]{1,0:T(8,128)(2,1)}, u32[]{:S(2)}, u32[]{:S(2)}) collective-permute-start(bf16[24,3072]{1,0:T(8,128)(2,1)} %pad_maximum_fusion.10), channel_id=1, source_target_pairs={{0,3},{1,0},{2,1},{3,2},{4,7},{5,4},{6,5},{7,6},{8,11},{9,8},{10,9... | collective-permute-start | bytes 442376 | tf_op jit(solution)/shard_map/ppermute | solution.py:46
  59.0 16.4 %collective-permute-start.17 = (bf16[24,3072]{1,0:T(8,128)(2,1)}, bf16[24,3072]{1,0:T(8,128)(2,1)}, u32[]{:S(2)}, u32[]{:S(2)}) collective-permute-start(bf16[24,3072]{1,0:T(8,128)(2,1)} %pad_maximum_fusion.10), channel_id=1, source_target_pairs={{0,2},{1,3},{2,0},{3,1},{4,6},{5,7},{6,4},{7,5},{8,10},{9,11},{10,... | collective-permute-start | bytes 442376 | tf_op jit(solution)/shard_map/ppermute | solution.py:46
  59.9 15.5 %collective-permute-start.16 = (bf16[24,3072]{1,0:T(8,128)(2,1)}, bf16[24,3072]{1,0:T(8,128)(2,1)}, u32[]{:S(2)}, u32[]{:S(2)}) collective-permute-start(bf16[24,3072]{1,0:T(8,128)(2,1)} %pad_maximum_fusion.10), channel_id=1, source_target_pairs={{0,1},{1,2},{2,3},{3,0},{4,5},{5,6},{6,7},{7,4},{8,9},{9,10},{10,1... | collective-permute-start | bytes 442376 | tf_op jit(solution)/shard_map/ppermute | solution.py:46
  92.0 21.6 %collective-permute-start.25 = (bf16[2,192,1664]{2,1,0:T(8,128)(2,1)S(1)}, bf16[2,192,1664]{2,1,0:T(8,128)(2,1)S(1)}, u32[]{:S(2)}, u32[]{:S(2)}) collective-permute-start(bf16[2,192,1664]{2,1,0:T(8,128)(2,1)S(1)} %pad_maximum_fusion.refs_0_), channel_id=1, source_target_pairs={{0,4},{4,0},{8,12},{12,8},{16,20},{20,16},{24,28},{28,24},{1,5},{5... | collective-permute-start | bytes 3833864 | tf_op jit(solution)/shard_map/ppermute | solution.py:30
  97.4 17.3 %collective-permute-start.24 = (bf16[2,192,1664]{2,1,0:T(8,128)(2,1)S(1)}, bf16[2,192,1664]{2,1,0:T(8,128)(2,1)S(1)}, u32[]{:S(2)}, u32[]{:S(2)}) collective-permute-start(bf16[2,192,1664]{2,1,0:T(8,128)(2,1)S(1)} %pad_maximum_fusion.refs_0_), channel_id=1, source_target_pairs={{0,16},{4,12},{8,24},{12,4},{16,0},{20,28},{24,8},{28,20},{1,17},{... | collective-permute-start | bytes 3833864 | tf_op jit(solution)/shard_map/ppermute | solution.py:41
  153.1 16.9 %collective-permute-start.30 = (bf16[4,384,768]{2,1,0:T(8,128)(2,1)}, bf16[4,384,768]{2,1,0:T(8,128)(2,1)S(1)}, u32[]{:S(2)}, u32[]{:S(2)}) collective-permute-start(bf16[4,384,768]{2,1,0:T(8,128)(2,1)} %get-tuple-element.207), channel_id=1, source_target_pairs={{0,4},{4,0},{8,12},{12,8},{16,20},{20,16},{24,28},{28,24},{1,5},{5... | collective-permute-start | bytes 7077896 | tf_op jit(solution)/shard_map/ppermute | solution.py:30
  154.6 15.4 %collective-permute-start.28 = (bf16[128,1536]{1,0:T(8,128)(2,1)}, bf16[128,1536]{1,0:T(8,128)(2,1)S(1)}, u32[]{:S(2)}, u32[]{:S(2)}) collective-permute-start(bf16[128,1536]{1,0:T(8,128)(2,1)} %get-tuple-element.206), channel_id=1, source_target_pairs={{4,0},{5,1},{6,2},{7,3},{12,8},{13,9},{14,10},{15,11},{20,16},{21,... | collective-permute-start | bytes 1179656 | tf_op jit(solution)/shard_map/ppermute | solution.py:1133
  155.8 14.2 %collective-permute-start.29 = (bf16[256,768]{1,0:T(8,128)(2,1)S(1)}, bf16[256,768]{1,0:T(8,128)(2,1)S(1)}, u32[]{:S(2)}, u32[]{:S(2)}) collective-permute-start(bf16[256,768]{1,0:T(8,128)(2,1)S(1)} %get-tuple-element.303), channel_id=1, source_target_pairs={{2,0},{0,1},{6,2},{4,3},{3,4},{1,5},{7,6},{5,7},{10,8},{8,9},{14,1... | collective-permute-start | bytes 1179656 | tf_op jit(solution)/shard_map/ppermute | solution.py:95
  174.2 20.8 %collective-permute-start.32 = (bf16[2,384,768]{2,1,0:T(8,128)(2,1)}, bf16[2,384,768]{2,1,0:T(8,128)(2,1)S(1)}, u32[]{:S(2)}, u32[]{:S(2)}) collective-permute-start(bf16[2,384,768]{2,1,0:T(8,128)(2,1)} %shard_map.222), channel_id=1, source_target_pairs={{0,8},{4,20},{8,0},{12,28},{16,24},{20,4},{24,16},{28,12},{1,9},{5... | collective-permute-start | bytes 3538952 | tf_op jit(solution)/shard_map/ppermute | solution.py:41
  175.9 19.1 %collective-permute-start.31 = (bf16[2,128,768]{2,1,0:T(8,128)(2,1)S(1)}, bf16[2,128,768]{2,1,0:T(8,128)(2,1)S(1)}, u32[]{:S(2)}, u32[]{:S(2)}) collective-permute-start(bf16[2,128,768]{2,1,0:T(8,128)(2,1)S(1)} %get-tuple-element.300), channel_id=1, source_target_pairs={{0,4},{4,0},{8,12},{12,8},{16,20},{20,16},{24,28},{28,24},{1,5},{5... | collective-permute-start | bytes 1179656 | tf_op jit(solution)/shard_map/ppermute | solution.py:30
  195.1 19.3 %collective-permute-start.34 = (bf16[2,2,128,768]{3,2,1,0:T(8,128)(2,1)S(1)}, bf16[2,2,128,768]{3,2,1,0:T(8,128)(2,1)S(1)}, u32[]{:S(2)}, u32[]{:S(2)}) collective-permute-start(bf16[2,2,128,768]{3,2,1,0:T(8,128)(2,1)S(1)} %pad_maximum_fusion.2.pair_ref), channel_id=1, source_target_pairs={{0,8},{4,20},{8,0},{12,28},{16,24},{20,4},{24,16},{28,12},{1,9},{5... | collective-permute-start | bytes 2359304 | tf_op jit(solution)/shard_map/ppermute | solution.py:41
  199.1 15.3 %collective-permute-start.35 = (bf16[1,384,768]{2,1,0:T(8,128)(2,1)}, bf16[1,384,768]{2,1,0:T(8,128)(2,1)S(1)}, u32[]{:S(2)}, u32[]{:S(2)}) collective-permute-start(bf16[1,384,768]{2,1,0:T(8,128)(2,1)} %shard_map.224), channel_id=1, source_target_pairs={{0,16},{4,12},{8,24},{12,4},{16,0},{20,28},{24,8},{28,20},{1,17},{... | collective-permute-start | bytes 1769480 | tf_op jit(solution)/shard_map/ppermute | solution.py:41
  201.4 12.9 %collective-permute-start.37 = (f32[8,1920]{1,0:T(8,128)S(1)}, f32[8,1920]{1,0:T(8,128)S(1)}, u32[]{:S(2)}, u32[]{:S(2)}) collective-permute-start(f32[8,1920]{1,0:T(8,128)S(1)} %add.113), channel_id=1, source_target_pairs={{0,1},{1,0},{2,3},{3,2},{4,5},{5,4},{6,7},{7,6},{8,9},{9,8},{10,11... | collective-permute-start | bytes 184328 | tf_op jit(solution)/shard_map/ppermute | solution.py:267
  215.3 22.0 %collective-permute-start.43 = (bf16[4,96,1920]{2,1,0:T(8,128)(2,1)}, bf16[4,96,1920]{2,1,0:T(8,128)(2,1)S(1)}, u32[]{:S(2)}, u32[]{:S(2)}) collective-permute-start(bf16[4,96,1920]{2,1,0:T(8,128)(2,1)} %get-tuple-element.241), channel_id=1, source_target_pairs={{0,4},{4,0},{8,12},{12,8},{16,20},{20,16},{24,28},{28,24},{1,5},{5... | collective-permute-start | bytes 4423688 | tf_op jit(solution)/shard_map/ppermute | solution.py:30
  217.9 19.5 %collective-permute-start.38 = (bf16[2,2,128,768]{3,2,1,0:T(8,128)(2,1)}, bf16[2,2,128,768]{3,2,1,0:T(8,128)(2,1)S(1)}, u32[]{:S(2)}, u32[]{:S(2)}) collective-permute-start(bf16[2,2,128,768]{3,2,1,0:T(8,128)(2,1)} %shard_map.226), channel_id=1, source_target_pairs={{0,16},{4,12},{8,24},{12,4},{16,0},{20,28},{24,8},{28,20},{1,17},{... | collective-permute-start | bytes 2359304 | tf_op jit(solution)/shard_map/ppermute | solution.py:41
  223.5 13.3 %collective-permute-start.39 = (bf16[96,768]{1,0:T(8,128)(2,1)}, bf16[96,768]{1,0:T(8,128)(2,1)S(1)}, u32[]{:S(2)}, u32[]{:S(2)}) collective-permute-start(bf16[96,768]{1,0:T(8,128)(2,1)} %get-tuple-element.237), channel_id=1, source_target_pairs={{0,1},{1,2},{2,3},{3,0},{4,5},{5,6},{6,7},{7,4},{8,9},{9,10},{10,1... | collective-permute-start | bytes 442376 | tf_op jit(solution)/shard_map/ppermute | solution.py:46
  244.5 23.5 %collective-permute-start.48 = (bf16[256,768]{1,0:T(8,128)(2,1)S(1)}, bf16[256,768]{1,0:T(8,128)(2,1)S(1)}, u32[]{:S(2)}, u32[]{:S(2)}) collective-permute-start(bf16[256,768]{1,0:T(8,128)(2,1)S(1)} %get-tuple-element.297), channel_id=1, source_target_pairs={{2,0},{0,1},{6,2},{4,3},{3,4},{1,5},{7,6},{5,7},{10,8},{8,9},{14,1... | collective-permute-start | bytes 1179656 | tf_op jit(solution)/shard_map/ppermute | solution.py:95
  262.3 18.5 %collective-permute-start.44 = (bf16[2,128,768]{2,1,0:T(8,128)(2,1)}, bf16[2,128,768]{2,1,0:T(8,128)(2,1)S(1)}, u32[]{:S(2)}, u32[]{:S(2)}) collective-permute-start(bf16[2,128,768]{2,1,0:T(8,128)(2,1)} %get-tuple-element.243), channel_id=1, source_target_pairs={{0,4},{4,0},{8,12},{12,8},{16,20},{20,16},{24,28},{28,24},{1,5},{5... | collective-permute-start | bytes 1179656 | tf_op jit(solution)/shard_map/ppermute | solution.py:30
  (82 other events, 500.2 us)

commit v2 on v1

--- a/solution.py
+++ b/solution.py
@@ -528,13 +528,20 @@
 
     tall = 3 * HALO if total % (3 * HALO) == 0 else HALO
 
+    model = x_ref.shape[1]
+
+    def scaled(i, carry):
+        at = pl.ds(pl.multiple_of(i * tall, tall), tall)
+        u = x_ref[at, :].astype(F32)
+        proj_ref[at, 0:model] = u * lax.rsqrt(jnp.mean(u * u, axis=1, keepdims=True) + EPSILON)
+        return carry
+
     def norm(i, carry):
         at = pl.ds(pl.multiple_of(i * tall, tall), tall)
-        u = x_ref[at, :].astype(F32)
-        scale = lax.rsqrt(jnp.mean(u * u, axis=1, keepdims=True) + EPSILON)
-        nh_ref[at, :] = (u * scale * gain).astype(BF16)
-        return carry
-
+        nh_ref[at, :] = (proj_ref[at, 0:model] * gain).astype(BF16)
+        return carry
+
+    lax.fori_loop(0, total // tall, scaled, 0)
     wait_all(copies)
     gain = gain_row(w_ref)
     lax.fori_loop(0, total // tall, norm, 0)
@@ -985,10 +992,20 @@
 def token_back_kernel(plan, rows, scal, gproj_ref, gng_ref, x_ref, c_ref, *refs):
     count = PIECES
     pieces = refs[:count]
-    gtok_ref, w_ref, acc_ref, sem = refs[count:]
+    gtok_ref, w_ref, acc_ref, hat_ref, scale_ref, sem = refs[count:]
     copies = start_pieces(scal[0], pieces, plan, w_ref, sem, rows)
     length, model = c_ref.shape
     tall = 4 * HALO
+
+    def scaled(i, carry):
+        at = pl.ds(pl.multiple_of(i * tall, tall), tall)
+        u = x_ref[pl.ds(pl.multiple_of(i * tall + HALO, HALO), tall), :].astype(F32)
+        scale = lax.rsqrt(jnp.mean(u * u, axis=1, keepdims=True) + EPSILON)
+        hat_ref[at, :] = u * scale
+        scale_ref[at, :] = jnp.broadcast_to(scale, (tall, LANES))
+        return carry
+
+    lax.fori_loop(0, length // tall, scaled, 0)
     wait_all(copies)
     for j in range(2):
         cols = slice(j * model // 2, (j + 1) * model // 2)
@@ -997,11 +1014,9 @@
 
     def norm_back(i, carry):
         at = pl.ds(pl.multiple_of(i * tall, tall), tall)
-        u = x_ref[pl.ds(pl.multiple_of(i * tall + HALO, HALO), tall), :].astype(F32)
-        scale = lax.rsqrt(jnp.mean(u * u, axis=1, keepdims=True) + EPSILON)
-        nh = u * scale
+        nh = hat_ref[at, :]
         g = acc_ref[at, :] * gain
-        grads = scale * (g - nh * jnp.mean(g * nh, axis=1, keepdims=True))
+        grads = scale_ref[at, 0:1] * (g - nh * jnp.mean(g * nh, axis=1, keepdims=True))
         gtok_ref[at, :] = (grads + c_ref[at, :].astype(F32)).astype(BF16)
         return carry
 
@@ -1241,7 +1256,8 @@
             [gproj, gng, x_ext, c_own],
             conv_pieces,
             [((length, model), BF16)],
-            [pltpu.VMEM((model, WIDTH), BF16), pltpu.VMEM((length, model), F32), sems(conv_plan)],
+            [pltpu.VMEM((model, WIDTH), BF16), pltpu.VMEM((length, model), F32), pltpu.VMEM((length, model), F32),
+             pltpu.VMEM((length, LANES), F32), sems(conv_plan)],
         ),
         *moving,
     )

time: 287 us -> 286 us (level)
  transfers between devices with their start and end apart: 54 -> 54, of which waited for: 13 -> 12; matrix products, arithmetic and copies ran while one was open for 7% -> 7% of each run, Pallas kernels for 39% -> 38%
where the time goes in v2:
time: 286 us; the launch traced here: 285 us
  Pallas kernels  136 us (48%)
  starting transfers between devices  73.3 us (26%)
  waiting for transfers between devices  35.3 us (12%)
  local copies, waits for them, and re-layouts  20.3 us (7%)
  other arithmetic  17.6 us (6%)
    pallas_call x9, Pallas kernels, call(): pl.pallas_call(body, out_shape=[jax.ShapeDtypeStruct(shape, kind) for sha...  110 us
    ppermute x12, starting transfers between devices, shift_seq(): lax.ppermute(value, 'seq', [(i, (i + step) % size) for i in range(size)])  20.6 us
    ppermute x16, starting transfers between devices, flip_dp(): return lax.ppermute(value, 'dp', pairs)  14.3 us
    ppermute x12, starting transfers between devices, flip_step(): return lax.ppermute(value, 'dp', pairs)  14.3 us
    ppermute x16, waiting for transfers between devices, flip_dp(): return lax.ppermute(value, 'dp', pairs)  12.5 us
    pallas_call x4, Pallas kernels, pick(): pl.pallas_call(body, out_shape=[jax.ShapeDtypeStruct(shape, BF16) for sha...  10.2 us
    unnamed x102, local copies, waits for them, and re-layouts  9.78 us
    pallas_call x4, Pallas kernels, give_up(): pl.pallas_call(give_kernel, grid=(first,), out_shape=jax.ShapeDtypeStruct...  9.42 us
  transfers between devices with their start and end apart: 54, of which 12 were waited for; matrix products, arithmetic and copies ran while one was open for 7% of the time, Pallas kernels for 38%

profile of v2, /device:TPU:0, one launch (start us, length us, event | category | flops | bytes accessed | tf_op | source)
XLA Modules:
  0.0 285.1 jit_solution(8904739556552307851)
XLA Ops:
  3.4 5.1 %collective-permute-start.5 = (bf16[24,1920]{1,0:T(8,128)(2,1)S(1)}, bf16[24,1920]{1,0:T(8,128)(2,1)S(1)}, u32[]{:S(2)}, u32[]{:S(2)}) collective-permute-start(bf16[24,1920]{1,0:T(8,128)(2,1)S(1)} %pad.19), channel_id=1, source_target_pairs={{0,3},{1,0},{2,1},{3,2},{4,7},{5,4},{6,5},{7,6},{8,11},{9,8},{10,9... | collective-permute-start | bytes 276488 | tf_op jit(solution)/shard_map/ppermute | solution.py:46
  24.8 8.0 %collective-permute-done.1 = s32[2,4]{1,0:T(2,128)S(1)} collective-permute-done((s32[2,4]{1,0:T(2,128)S(1)}, s32[2,4]{1,0:T(2,128)S(1)}, u32[]{:S(2)}, u32[]{:S(2)}) %collective-permute-start.1) | collective-permute-done | bytes 64 | tf_op jit(solution)/shard_map/ppermute | solution.py:30
  52.2 2.8 collective-permute-done.12.refs_1_
  62.0 12.4 %shard_map.214 = (bf16[528,768]{1,0:T(8,128)(2,1)}, bf16[528,768]{1,0:T(8,128)(2,1)}, bf16[528,1792]{1,0:T(8,128)(2,1)}, bf16[512,1792]{1,0:T(8,128)(2,1)}, f32[...) custom-call(s32[3]{0:T(128)} %pad_add_fusion.4.scal, bf16[256,768]{1,0:T(8,128)(2,1)} %copy-done.23, ...), custom_call_target="tpu_custom_call" | custom-call | tf_op jit(solution)/shard_map/pallas_call | solution.py:1030
  75.3 2.7 shard_map.216
  82.6 7.6 %shard_map.215 = (f32[512,1536]{1,0:T(8,128)}, bf16[128,1536]{1,0:T(8,128)(2,1)}, f32[8,128]{1,0:T(8,128)}) custom-call(bf16[512,1792]{1,0:T(8,128)(2,1)} %get-tuple-element.170.act_ref, f32[512,128]{1,0:T(8,128)} %get-tuple-element.171.step_ref, f32[512,128]{1,0:T(8,128)} %get-tuple-element.172.cum_ref), custom_call_target="tpu_custom_call" | custom-call | tf_op jit(solution)/shard_map/pallas_call | solution.py:1030
  90.9 5.4 %collective-permute-start.25 = (bf16[2,192,1664]{2,1,0:T(8,128)(2,1)S(1)}, bf16[2,192,1664]{2,1,0:T(8,128)(2,1)S(1)}, u32[]{:S(2)}, u32[]{:S(2)}) collective-permute-start(bf16[2,192,1664]{2,1,0:T(8,128)(2,1)S(1)} %pad_maximum_fusion.refs_0_), channel_id=1, source_target_pairs={{0,4},{4,0},{8,12},{12,8},{16,20},{20,16},{24,28},{28,24},{1,5},{5... | collective-permute-start | bytes 3833864 | tf_op jit(solution)/shard_map/ppermute | solution.py:30
  97.3 2.9 %collective-permute-start.22 = (bf16[128,1536]{1,0:T(8,128)(2,1)S(1)}, bf16[128,1536]{1,0:T(8,128)(2,1)}, u32[]{:S(2)}, u32[]{:S(2)}) collective-permute-start(bf16[128,1536]{1,0:T(8,128)(2,1)S(1)} %copy-done.49), channel_id=1, source_target_pairs={{0,4},{1,5},{2,6},{3,7},{8,12},{9,13},{10,14},{11,15},{16,20},{17,... | collective-permute-start | bytes 1179656 | tf_op jit(solution)/shard_map/ppermute | solution.py:1148
  101.1 7.4 %shard_map.217 = (f32[512,1536]{1,0:T(8,128)}, bf16[4,128,1536]{2,1,0:T(8,128)(2,1)}) custom-call(f32[512,1536]{1,0:T(8,128)} %get-tuple-element.181.local_ref, bf16[512,1792]{1,0:T(8,128)(2,1)} %get-tuple-element.170.act_ref, f32[512,128]{1,0:T(8,128)} %get-tuple-element.171.step_ref, f32[512,128]{1,0:T(8,128)} %get-tuple-element.172.cum_ref, ...), custom_call_target="tpu_custom_call" | custom-call | tf_op jit(solution)/shard_map/pallas_call | solution.py:1030
  108.5 4.1 %collective-permute-done.23.two_ref = bf16[256,768]{1,0:T(8,128)(2,1)} collective-permute-done((bf16[256,768]{1,0:T(8,128)(2,1)}, bf16[256,768]{1,0:T(8,128)(2,1)}, u32[]{:S(2)}, u32[]{:S(2)}) %collective-permute-start.23) | collective-permute-done | bytes 393248 | tf_op jit(solution)/shard_map/ppermute | solution.py:85
  113.6 3.0 %collective-permute-done.26.refs_3_ = bf16[2,192,1664]{2,1,0:T(8,128)(2,1)S(1)} collective-permute-done((bf16[2,192,1664]{2,1,0:T(8,128)(2,1)S(1)}, bf16[2,192,1664]{2,1,0:T(8,128)(2,1)S(1)}, u32[]{:S(2)}, u32[]{:S(2)}) %collective-permute-start.26) | collective-permute-done | bytes 1277984 | tf_op jit(solution)/shard_map/ppermute | solution.py:30
  117.7 21.8 %shard_map.218 = (bf16[512,768]{1,0:T(8,128)(2,1)}, bf16[512,768]{1,0:T(8,128)(2,1)}, bf16[512,1536]{1,0:T(8,128)(2,1)}, bf16[512,1536]{1,0:T(8,128)(2,1)}, bf16...) custom-call(s32[3]{0:T(128)} %pad_add_fusion.4.scal, ...), custom_call_target="tpu_custom_call" | custom-call | tf_op jit(solution)/shard_map/pallas_call | solution.py:1030
  141.3 10.7 %shard_map.219 = (bf16[4,384,768]{2,1,0:T(8,128)(2,1)}, bf16[4,384,768]{2,1,0:T(8,128)(2,1)}) custom-call(s32[3]{0:T(128)} %pad_add_fusion.4.scal, bf16[512,1536]{1,0:T(8,128)(2,1)} %get-tuple-element.194.gn_ref, bf16[512,768]{1,0:T(8,128)(2,1)} %get-tuple-element.195.c_ref, bf16[528,768]{1,0:T(8,128)(2,1)} %get-tuple-element.187.nh_ref, ...), custom_call_target="tpu_custom_call" | custom-call | tf_op jit(solution)/shard_map/pallas_call | solution.py:1030
  156.6 12.3 %shard_map.220 = (f32[512,1536]{1,0:T(8,128)}, f32[512,256]{1,0:T(8,128)}, f32[512,768]{1,0:T(8,128)}) custom-call(s32[3]{0:T(128)} %pad_add_fusion.4.scal, bf16[512,1792]{1,0:T(8,128)(2,1)} %get-tuple-element.170.act_ref, f32[512,128]{1,0:T(8,128)} %get-tuple-element.171.step_ref, f32[512,128]{1,0:T(8,128)} %get-tuple-element.172.cum_ref, ...), custom_call_target="tpu_custom_call" | custom-call | tf_op jit(solution)/shard_map/pallas_call | solution.py:1030
  174.9 19.0 %shard_map.221 = (f32[512,1792]{1,0:T(8,128)}, f32[16,1792]{1,0:T(8,128)}, bf16[512,128]{1,0:T(8,128)(2,1)}, f32[8,1920]{1,0:T(8,128)}) custom-call(bf16[512,1792]{1,0:T(8,128)(2,1)} %get-tuple-element.170.act_ref, f32[512,128]{1,0:T(8,128)} %get-tuple-element.171.step_ref, f32[512,128]{1,0:T(8,128)} %get-tuple-element.210.sig_ref, ...), custom_call_target="tpu_custom_call" | custom-call | tf_op jit(solution)/shard_map/pallas_call | solution.py:1030
  203.1 10.2 %shard_map.223 = (bf16[512,1920]{1,0:T(8,128)(2,1)}, bf16[4,96,1920]{2,1,0:T(8,128)(2,1)}, bf16[4,96,1920]{2,1,0:T(8,128)(2,1)}) custom-call(s32[3]{0:T(128)} %pad_add_fusion.4.scal, f32[512,1792]{1,0:T(8,128)} %get-tuple-element.225.gconv_ref, f32[16,1792]{1,0:T(8,128)} %copy-done.40, bf16[512,128]{1,0:T(8,128)(2,1)} %get-tuple-element.227.graw_ref, ...), custom_call_target="tpu_custom_call" | custom-call | tf_op jit(solution)/shard_map/pallas_call | solution.py:1030
  220.2 2.9 %shard_map.227 = (f32[96,768]{1,0:T(8,128)}, bf16[96,768]{1,0:T(8,128)(2,1)}, bf16[96,768]{1,0:T(8,128)(2,1)}, bf16[96,768]{1,0:T(8,128)(2,1)}) custom-call(s32[1]{0:T(128)} %bitcast.39.seq_ref, bf16[4,384,768]{2,1,0:T(8,128)(2,1)} %get-tuple-element.222.refs_0_, bf16[4,384,768]{2,1,0:T(8,128)(2,1)} %copy-done, bf16[2,384,768]{2,1,0:T(8,128)(2,1)} %copy-done.8, ...), custom_call_target="tpu_custom_call" | custom-call | tf_op jit(solution)/shard_map/pallas_call | solution.py:244
  226.9 8.6 %shard_map.225 = bf16[512,768]{1,0:T(8,128)(2,1)} custom-call(s32[3]{0:T(128)} %pad_add_fusion.4.scal, bf16[512,1920]{1,0:T(8,128)(2,1)} %get-tuple-element.234.gproj_ref, f32[512,768]{1,0:T(8,128)} %get-tuple-element.235.gng_ref, bf16[528,768]{1,0:T(8,128)(2,1)} %get-tuple-element.188.x_ref, bf16[512,768]{1,0:T(8,128)(2,1)} %get-tuple-element.195.c_ref, ...), custom_call_target="tpu_custom_call" | custom-call | tf_op jit(solution)/shard_map/pallas_call | solution.py:1030
  243.8 4.9 %collective-permute-start.48 = (bf16[256,768]{1,0:T(8,128)(2,1)S(1)}, bf16[256,768]{1,0:T(8,128)(2,1)S(1)}, u32[]{:S(2)}, u32[]{:S(2)}) collective-permute-start(bf16[256,768]{1,0:T(8,128)(2,1)S(1)} %get-tuple-element.297), channel_id=1, source_target_pairs={{2,0},{0,1},{6,2},{4,3},{3,4},{1,5},{7,6},{5,7},{10,8},{8,9},{14,1... | collective-permute-start | bytes 1179656 | tf_op jit(solution)/shard_map/ppermute | solution.py:95
  248.6 4.4 %collective-permute-done.47.refs_2_ = bf16[2,96,1920]{2,1,0:T(8,128)(2,1)S(1)} collective-permute-done((bf16[2,96,1920]{2,1,0:T(8,128)(2,1)}, bf16[2,96,1920]{2,1,0:T(8,128)(2,1)S(1)}, u32[]{:S(2)}, u32[]{:S(2)}) %collective-permute-start.47) | collective-permute-done | bytes 737312 | tf_op jit(solution)/shard_map/ppermute | solution.py:41
  259.4 2.7 shard_map.228
  262.1 5.4 %collective-permute-done.48 = bf16[256,768]{1,0:T(8,128)(2,1)S(1)} collective-permute-done((bf16[256,768]{1,0:T(8,128)(2,1)S(1)}, bf16[256,768]{1,0:T(8,128)(2,1)S(1)}, u32[]{:S(2)}, u32[]{:S(2)}) %collective-permute-start.48) | collective-permute-done | bytes 393248 | tf_op jit(solution)/shard_map/ppermute | solution.py:95
  271.3 4.0 %collective-permute-start.51 = (bf16[24,1920]{1,0:T(8,128)(2,1)}, bf16[24,1920]{1,0:T(8,128)(2,1)S(1)}, u32[]{:S(2)}, u32[]{:S(2)}) collective-permute-start(bf16[24,1920]{1,0:T(8,128)(2,1)} %get-tuple-element.251), channel_id=1, source_target_pairs={{0,1},{1,2},{2,3},{3,0},{4,5},{5,6},{6,7},{7,4},{8,9},{9,10},{10,1... | collective-permute-start | bytes 276488 | tf_op jit(solution)/shard_map/ppermute | solution.py:46
  279.9 2.7 collective-permute-done.52
  (276 shorter events, 112.1 us)
Async XLA Ops:
  3.4 12.8 %collective-permute-start.5 = (bf16[24,1920]{1,0:T(8,128)(2,1)S(1)}, bf16[24,1920]{1,0:T(8,128)(2,1)S(1)}, u32[]{:S(2)}, u32[]{:S(2)}) collective-permute-start(bf16[24,1920]{1,0:T(8,128)(2,1)S(1)} %pad.19), channel_id=1, source_target_pairs={{0,3},{1,0},{2,1},{3,2},{4,7},{5,4},{6,5},{7,6},{8,11},{9,8},{10,9... | collective-permute-start | bytes 276488 | tf_op jit(solution)/shard_map/ppermute | solution.py:46
  10.2 13.0 %collective-permute-start = (s32[1,4]{1,0:T(1,128)S(1)}, s32[1,4]{1,0:T(1,128)S(1)}, u32[]{:S(2)}, u32[]{:S(2)}) collective-permute-start(s32[1,4]{1,0:T(1,128)S(1)} %add_bitcast_fusion), channel_id=1, source_target_pairs={{0,4},{4,0},{8,12},{12,8},{16,20},{20,16},{24,28},{28,24},{1,5},{5... | collective-permute-start | bytes 56 | tf_op jit(solution)/shard_map/ppermute | solution.py:30
  16.8 24.5 %collective-permute-start.10 = (bf16[2,2,128,768]{3,2,0,1:T(8,128)(2,1)S(1)}, bf16[2,2,128,768]{3,2,0,1:T(8,128)(2,1)S(1)}, u32[]{:S(2)}, u32[]{:S(2)}) collective-permute-start(bf16[2,2,128,768]{3,2,0,1:T(8,128)(2,1)S(1)} %pad_maximum_fusion.1), channel_id=1, source_target_pairs={{0,8},{4,20},{8,0},{12,28},{16,24},{20,4},{24,16},{28,12},{1,9},{5... | collective-permute-start | bytes 2359304 | tf_op jit(solution)/shard_map/ppermute | solution.py:41
  18.5 22.7 %collective-permute-start.9 = (bf16[1,96,1920]{2,1,0:T(8,128)(2,1)S(1)}, bf16[1,96,1920]{2,1,0:T(8,128)(2,1)}, u32[]{:S(2)}, u32[]{:S(2)}) collective-permute-start(bf16[1,96,1920]{2,1,0:T(8,128)(2,1)S(1)} %bitcast.78), channel_id=1, source_target_pairs={{0,8},{4,20},{8,0},{12,28},{16,24},{20,4},{24,16},{28,12},{1,9},{5... | collective-permute-start | bytes 1105928 | tf_op jit(solution)/shard_map/ppermute | solution.py:41
  19.1 22.1 %collective-permute-start.7 = (bf16[256,768]{1,0:T(8,128)(2,1)}, bf16[256,768]{1,0:T(8,128)(2,1)S(1)}, u32[]{:S(2)}, u32[]{:S(2)}) collective-permute-start(bf16[256,768]{1,0:T(8,128)(2,1)} %get-tuple-element.139), channel_id=1, source_target_pairs={{0,0},{1,2},{2,4},{3,6},{4,1},{5,3},{6,5},{7,7},{8,8},{9,10},{10,1... | collective-permute-start | bytes 1179656 | tf_op jit(solution)/shard_map/ppermute | solution.py:85
  20.7 20.5 %collective-permute-start.8 = (bf16[256,768]{1,0:T(8,128)(2,1)S(1)}, bf16[256,768]{1,0:T(8,128)(2,1)S(1)}, u32[]{:S(2)}, u32[]{:S(2)}) collective-permute-start(bf16[256,768]{1,0:T(8,128)(2,1)S(1)} %get-tuple-element.140), channel_id=1, source_target_pairs={{0,2},{1,0},{2,6},{3,4},{4,3},{5,1},{6,7},{7,5},{8,10},{9,8},{10,1... | collective-permute-start | bytes 1179656 | tf_op jit(solution)/shard_map/ppermute | solution.py:85
  55.0 19.3 %collective-permute-start.15 = (bf16[2,2,128,768]{3,2,1,0:T(8,128)(2,1)}, bf16[2,2,128,768]{3,2,1,0:T(8,128)(2,1)S(1)}, u32[]{:S(2)}, u32[]{:S(2)}) collective-permute-start(bf16[2,2,128,768]{3,2,1,0:T(8,128)(2,1)} %shard_map.213), channel_id=1, source_target_pairs={{0,16},{4,12},{8,24},{12,4},{16,0},{20,28},{24,8},{28,20},{1,17},{... | collective-permute-start | bytes 2359304 | tf_op jit(solution)/shard_map/ppermute | solution.py:41
  56.6 17.8 %collective-permute-start.18 = (bf16[24,3072]{1,0:T(8,128)(2,1)}, bf16[24,3072]{1,0:T(8,128)(2,1)}, u32[]{:S(2)}, u32[]{:S(2)}) collective-permute-start(bf16[24,3072]{1,0:T(8,128)(2,1)} %pad_maximum_fusion.10), channel_id=1, source_target_pairs={{0,3},{1,0},{2,1},{3,2},{4,7},{5,4},{6,5},{7,6},{8,11},{9,8},{10,9... | collective-permute-start | bytes 442376 | tf_op jit(solution)/shard_map/ppermute | solution.py:46
  59.0 15.4 %collective-permute-start.17 = (bf16[24,3072]{1,0:T(8,128)(2,1)}, bf16[24,3072]{1,0:T(8,128)(2,1)}, u32[]{:S(2)}, u32[]{:S(2)}) collective-permute-start(bf16[24,3072]{1,0:T(8,128)(2,1)} %pad_maximum_fusion.10), channel_id=1, source_target_pairs={{0,2},{1,3},{2,0},{3,1},{4,6},{5,7},{6,4},{7,5},{8,10},{9,11},{10,... | collective-permute-start | bytes 442376 | tf_op jit(solution)/shard_map/ppermute | solution.py:46
  59.9 14.4 %collective-permute-start.16 = (bf16[24,3072]{1,0:T(8,128)(2,1)}, bf16[24,3072]{1,0:T(8,128)(2,1)}, u32[]{:S(2)}, u32[]{:S(2)}) collective-permute-start(bf16[24,3072]{1,0:T(8,128)(2,1)} %pad_maximum_fusion.10), channel_id=1, source_target_pairs={{0,1},{1,2},{2,3},{3,0},{4,5},{5,6},{6,7},{7,4},{8,9},{9,10},{10,1... | collective-permute-start | bytes 442376 | tf_op jit(solution)/shard_map/ppermute | solution.py:46
  90.9 21.6 %collective-permute-start.25 = (bf16[2,192,1664]{2,1,0:T(8,128)(2,1)S(1)}, bf16[2,192,1664]{2,1,0:T(8,128)(2,1)S(1)}, u32[]{:S(2)}, u32[]{:S(2)}) collective-permute-start(bf16[2,192,1664]{2,1,0:T(8,128)(2,1)S(1)} %pad_maximum_fusion.refs_0_), channel_id=1, source_target_pairs={{0,4},{4,0},{8,12},{12,8},{16,20},{20,16},{24,28},{28,24},{1,5},{5... | collective-permute-start | bytes 3833864 | tf_op jit(solution)/shard_map/ppermute | solution.py:30
  96.3 17.3 %collective-permute-start.24 = (bf16[2,192,1664]{2,1,0:T(8,128)(2,1)S(1)}, bf16[2,192,1664]{2,1,0:T(8,128)(2,1)S(1)}, u32[]{:S(2)}, u32[]{:S(2)}) collective-permute-start(bf16[2,192,1664]{2,1,0:T(8,128)(2,1)S(1)} %pad_maximum_fusion.refs_0_), channel_id=1, source_target_pairs={{0,16},{4,12},{8,24},{12,4},{16,0},{20,28},{24,8},{28,20},{1,17},{... | collective-permute-start | bytes 3833864 | tf_op jit(solution)/shard_map/ppermute | solution.py:41
  152.0 16.9 %collective-permute-start.30 = (bf16[4,384,768]{2,1,0:T(8,128)(2,1)}, bf16[4,384,768]{2,1,0:T(8,128)(2,1)S(1)}, u32[]{:S(2)}, u32[]{:S(2)}) collective-permute-start(bf16[4,384,768]{2,1,0:T(8,128)(2,1)} %get-tuple-element.207), channel_id=1, source_target_pairs={{0,4},{4,0},{8,12},{12,8},{16,20},{20,16},{24,28},{28,24},{1,5},{5... | collective-permute-start | bytes 7077896 | tf_op jit(solution)/shard_map/ppermute | solution.py:30
  154.4 14.5 %collective-permute-start.28 = (bf16[128,1536]{1,0:T(8,128)(2,1)}, bf16[128,1536]{1,0:T(8,128)(2,1)S(1)}, u32[]{:S(2)}, u32[]{:S(2)}) collective-permute-start(bf16[128,1536]{1,0:T(8,128)(2,1)} %get-tuple-element.206), channel_id=1, source_target_pairs={{4,0},{5,1},{6,2},{7,3},{12,8},{13,9},{14,10},{15,11},{20,16},{21,... | collective-permute-start | bytes 1179656 | tf_op jit(solution)/shard_map/ppermute | solution.py:1148
  155.7 13.2 %collective-permute-start.29 = (bf16[256,768]{1,0:T(8,128)(2,1)S(1)}, bf16[256,768]{1,0:T(8,128)(2,1)S(1)}, u32[]{:S(2)}, u32[]{:S(2)}) collective-permute-start(bf16[256,768]{1,0:T(8,128)(2,1)S(1)} %get-tuple-element.303), channel_id=1, source_target_pairs={{2,0},{0,1},{6,2},{4,3},{3,4},{1,5},{7,6},{5,7},{10,8},{8,9},{14,1... | collective-permute-start | bytes 1179656 | tf_op jit(solution)/shard_map/ppermute | solution.py:95
  173.1 20.8 %collective-permute-start.32 = (bf16[2,384,768]{2,1,0:T(8,128)(2,1)}, bf16[2,384,768]{2,1,0:T(8,128)(2,1)S(1)}, u32[]{:S(2)}, u32[]{:S(2)}) collective-permute-start(bf16[2,384,768]{2,1,0:T(8,128)(2,1)} %shard_map.222), channel_id=1, source_target_pairs={{0,8},{4,20},{8,0},{12,28},{16,24},{20,4},{24,16},{28,12},{1,9},{5... | collective-permute-start | bytes 3538952 | tf_op jit(solution)/shard_map/ppermute | solution.py:41
  174.8 19.1 %collective-permute-start.31 = (bf16[2,128,768]{2,1,0:T(8,128)(2,1)S(1)}, bf16[2,128,768]{2,1,0:T(8,128)(2,1)S(1)}, u32[]{:S(2)}, u32[]{:S(2)}) collective-permute-start(bf16[2,128,768]{2,1,0:T(8,128)(2,1)S(1)} %get-tuple-element.300), channel_id=1, source_target_pairs={{0,4},{4,0},{8,12},{12,8},{16,20},{20,16},{24,28},{28,24},{1,5},{5... | collective-permute-start | bytes 1179656 | tf_op jit(solution)/shard_map/ppermute | solution.py:30
  194.0 19.3 %collective-permute-start.34 = (bf16[2,2,128,768]{3,2,1,0:T(8,128)(2,1)S(1)}, bf16[2,2,128,768]{3,2,1,0:T(8,128)(2,1)S(1)}, u32[]{:S(2)}, u32[]{:S(2)}) collective-permute-start(bf16[2,2,128,768]{3,2,1,0:T(8,128)(2,1)S(1)} %pad_maximum_fusion.2.pair_ref), channel_id=1, source_target_pairs={{0,8},{4,20},{8,0},{12,28},{16,24},{20,4},{24,16},{28,12},{1,9},{5... | collective-permute-start | bytes 2359304 | tf_op jit(solution)/shard_map/ppermute | solution.py:41
  198.0 15.3 %collective-permute-start.35 = (bf16[1,384,768]{2,1,0:T(8,128)(2,1)}, bf16[1,384,768]{2,1,0:T(8,128)(2,1)S(1)}, u32[]{:S(2)}, u32[]{:S(2)}) collective-permute-start(bf16[1,384,768]{2,1,0:T(8,128)(2,1)} %shard_map.224), channel_id=1, source_target_pairs={{0,16},{4,12},{8,24},{12,4},{16,0},{20,28},{24,8},{28,20},{1,17},{... | collective-permute-start | bytes 1769480 | tf_op jit(solution)/shard_map/ppermute | solution.py:41
  200.4 12.9 %collective-permute-start.37 = (f32[8,1920]{1,0:T(8,128)S(1)}, f32[8,1920]{1,0:T(8,128)S(1)}, u32[]{:S(2)}, u32[]{:S(2)}) collective-permute-start(f32[8,1920]{1,0:T(8,128)S(1)} %add.113), channel_id=1, source_target_pairs={{0,1},{1,0},{2,3},{3,2},{4,5},{5,4},{6,7},{7,6},{8,9},{9,8},{10,11... | collective-permute-start | bytes 184328 | tf_op jit(solution)/shard_map/ppermute | solution.py:267
  214.3 22.3 %collective-permute-start.43 = (bf16[4,96,1920]{2,1,0:T(8,128)(2,1)}, bf16[4,96,1920]{2,1,0:T(8,128)(2,1)S(1)}, u32[]{:S(2)}, u32[]{:S(2)}) collective-permute-start(bf16[4,96,1920]{2,1,0:T(8,128)(2,1)} %get-tuple-element.241), channel_id=1, source_target_pairs={{0,4},{4,0},{8,12},{12,8},{16,20},{20,16},{24,28},{28,24},{1,5},{5... | collective-permute-start | bytes 4423688 | tf_op jit(solution)/shard_map/ppermute | solution.py:30
  216.8 19.8 %collective-permute-start.38 = (bf16[2,2,128,768]{3,2,1,0:T(8,128)(2,1)}, bf16[2,2,128,768]{3,2,1,0:T(8,128)(2,1)S(1)}, u32[]{:S(2)}, u32[]{:S(2)}) collective-permute-start(bf16[2,2,128,768]{3,2,1,0:T(8,128)(2,1)} %shard_map.226), channel_id=1, source_target_pairs={{0,16},{4,12},{8,24},{12,4},{16,0},{20,28},{24,8},{28,20},{1,17},{... | collective-permute-start | bytes 2359304 | tf_op jit(solution)/shard_map/ppermute | solution.py:41
  243.8 23.7 %collective-permute-start.48 = (bf16[256,768]{1,0:T(8,128)(2,1)S(1)}, bf16[256,768]{1,0:T(8,128)(2,1)S(1)}, u32[]{:S(2)}, u32[]{:S(2)}) collective-permute-start(bf16[256,768]{1,0:T(8,128)(2,1)S(1)} %get-tuple-element.297), channel_id=1, source_target_pairs={{2,0},{0,1},{6,2},{4,3},{3,4},{1,5},{7,6},{5,7},{10,8},{8,9},{14,1... | collective-permute-start | bytes 1179656 | tf_op jit(solution)/shard_map/ppermute | solution.py:95
  262.1 17.8 %collective-permute-start.44 = (bf16[2,128,768]{2,1,0:T(8,128)(2,1)}, bf16[2,128,768]{2,1,0:T(8,128)(2,1)S(1)}, u32[]{:S(2)}, u32[]{:S(2)}) collective-permute-start(bf16[2,128,768]{2,1,0:T(8,128)(2,1)} %get-tuple-element.243), channel_id=1, source_target_pairs={{0,4},{4,0},{8,12},{12,8},{16,20},{20,16},{24,28},{28,24},{1,5},{5... | collective-permute-start | bytes 1179656 | tf_op jit(solution)/shard_map/ppermute | solution.py:30
  (82 other events, 500.9 us)
